TPU v7x, 32 devices: a whole 2x2x4 slice. The times are simulated.
32 devices in a mesh: fsdp: 32 (over z, y, x, core).
Axes of the slice: x: 2, y: 2, z: 4, core: 2. Of those that a mesh axis runs over, the one named last changes fastest.
Arguments:
- tokens: bfloat16 [4096, 1024], P('fsdp'), may hold values from -6 to 6
- cotangent: bfloat16 [4096, 1024], P('fsdp'), may hold values from -6 to 6
- lengths: int32 [32, 4], P('fsdp'), may hold values from 0 to 128, as said below
- offsets: int32 [32, 4], P('fsdp'), may hold values from 0 to 128, as said below
- norm_mix: bfloat16 [1024], P('fsdp'), may hold values from 0.5 to 1.5
- w_query: bfloat16 [1024, 512], P('fsdp'), may hold values from -0.1875 to 0.1875
- w_key: bfloat16 [1024, 512], P('fsdp'), may hold values from -0.1875 to 0.1875
- w_value: bfloat16 [1024, 1024], P('fsdp'), may hold values from -0.1875 to 0.1875
- w_gate: bfloat16 [1024, 1024], P('fsdp'), may hold values from -0.1875 to 0.1875
- w_betadecay: bfloat16 [1024, 8], P('fsdp'), may hold values from -0.1875 to 0.1875
- conv_weight: bfloat16 [2048, 4], P('fsdp'), may hold values from -3 to 3
- out_gain: bfloat16 [256], P('fsdp'), may hold values from 0.5 to 1.5
- w_out: bfloat16 [1024, 1024], P('fsdp'), may hold values from -0.1875 to 0.1875
- norm_ffn: bfloat16 [1024], P('fsdp'), may hold values from 0.5 to 1.5
- w_ffgate: bfloat16 [1024, 2816], P('fsdp'), may hold values from -0.1875 to 0.1875
- w_ffup: bfloat16 [1024, 2816], P('fsdp'), may hold values from -0.1875 to 0.1875
- w_ffdown: bfloat16 [2816, 1024], P('fsdp'), may hold values from -0.109375 to 0.109375
- decay_params: float32 [2, 4], replicated, may hold values from -6.5 to 1
Outputs:
- output: bfloat16 [4096, 1024], P('fsdp')
- input_grad: float32 [4096, 1024], P('fsdp')
- grad_norm_mix: float32 [1024], P('fsdp')
- grad_query: float32 [1024, 512], P('fsdp')
- grad_key: float32 [1024, 512], P('fsdp')
- grad_value: float32 [1024, 1024], P('fsdp')
- grad_gate: float32 [1024, 1024], P('fsdp')
- grad_betadecay: float32 [1024, 8], P('fsdp')
- grad_conv: float32 [2048, 4], P('fsdp')
- grad_out_gain: float32 [256], P('fsdp')
- grad_out: float32 [1024, 1024], P('fsdp')
- grad_norm_ffn: float32 [1024], P('fsdp')
- grad_ffgate: float32 [1024, 2816], P('fsdp')
- grad_ffup: float32 [1024, 2816], P('fsdp')
- grad_ffdown: float32 [2816, 1024], P('fsdp')
- grad_decay: float32 [2, 4], replicated
Inputs may be any that keep to these rules, and one draw needn't show every extreme that they name: Row d lists the sequences packed in device d's 128 slots: entry s covers lengths[d, s] slots from slot offsets[d, s]. Used entries come first, in rising offset, without intersection, and each device has at least one; an unused entry has length 0 and offset 128. In every draw some device holds a single sequence of 128 slots. `offsets`: see lengths.
All inputs are finite; a program needn't handle non-finite values.
Results may differ from a plain program's by a relative error of at most 0.014.
The roundings to bfloat16 on the way count: a program that leaves them out, or rounds other values in their place, can miss the bound.
Values may be sent and summed in bfloat16 or wider, within the bound.
No kernel may reach another device: no remote copies, remote signals or barrier semaphores. Data moves between devices by JAX's collectives and lax.ppermute only.
A program may use at most 256 MiB of HBM per device.

v0:
```python
import jax
import jax.numpy as jnp
from jax import lax
from jax.experimental import pallas as pl
from jax.experimental.pallas import tpu as pltpu
from jax.sharding import PartitionSpec as P


H = 4
DK = 128
DV = 256
CONV = 4
KD = H * DK
VD = H * DV
QKV = 2 * KD + VD
SMALL = 128
F32 = jnp.float32
BF16 = jnp.bfloat16


def dot32(a, b, ca, cb):
    return lax.dot_general(
        a, b, (((ca,), (cb,)), ((), ())), preferred_element_type=F32, precision=lax.Precision.HIGHEST
    )


def mm(a, b):
    return jnp.dot(a, b, preferred_element_type=F32)


def mm_t(a, b):
    return lax.dot_general(a, b, (((1,), (1,)), ((), ())), preferred_element_type=F32)


def t_mm(a, b):
    return lax.dot_general(a, b, (((0,), (0,)), ((), ())), preferred_element_type=F32)


def sigmoid(v):
    return 1.0 / (1.0 + jnp.exp(-v))


def find_start(slot, len_ref, off_ref):
    start = slot
    for s in range(len_ref.shape[1]):
        first = off_ref[0, s]
        inside = (slot >= first) & (slot < first + len_ref[0, s])
        start = jnp.where(inside, first, start)
    return start


def conv_sum(pre, taps, keeps):
    total = pre * taps[CONV - 1 : CONV]
    for s in range(1, CONV):
        total = total + jnp.where(keeps[s], pltpu.roll(pre, s, 0), 0.0) * taps[CONV - 1 - s : CONV - s]
    return total


def conv_grad(pre, d_sum, taps, keeps):
    n = pre.shape[0]
    d_pre = d_sum * taps[CONV - 1 : CONV]
    d_taps = [None] * CONV
    d_taps[CONV - 1] = jnp.sum(d_sum * pre, axis=0, keepdims=True)
    for s in range(1, CONV):
        masked = jnp.where(keeps[s], d_sum, 0.0)
        d_pre = d_pre + pltpu.roll(masked, n - s, 0) * taps[CONV - 1 - s : CONV - s]
        d_taps[CONV - 1 - s] = jnp.sum(masked * pltpu.roll(pre, s, 0), axis=0, keepdims=True)
    return d_pre, d_taps


class Block:
    def __init__(self, len_ref, off_ref, bd, rate_row, shift_row):
        n = bd.shape[0]
        row = lax.broadcasted_iota(jnp.int32, (n, n), 0)
        col = lax.broadcasted_iota(jnp.int32, (n, n), 1)
        slot_c = lax.broadcasted_iota(jnp.int32, (n, 1), 0)
        slot_r = lax.broadcasted_iota(jnp.int32, (1, n), 1)
        start_c = find_start(slot_c, len_ref, off_ref)
        start_r = find_start(slot_r, len_ref, off_ref)
        same = start_c == start_r
        self.row, self.col = row, col
        self.low = same & (row >= col)
        self.strict = same & (row > col)
        self.keeps = [None] + [slot_c - s >= start_c for s in range(1, CONV)]
        self.low_f = jnp.where(self.low, 1.0, 0.0)
        self.beta = sigmoid(bd)
        shifted = bd + shift_row
        self.shifted = shifted
        self.soft = jnp.maximum(shifted, 0.0) + jnp.log1p(jnp.exp(-jnp.abs(shifted)))
        self.rate = jnp.exp(rate_row)
        self.logdecay = -self.rate * self.soft
        self.cum = dot32(self.low_f, self.logdecay, 1, 0)
        self.cum_t = self.cum.T

    def decay(self, h):
        gap = self.cum[:, H + h : H + h + 1] - self.cum_t[H + h : H + h + 1, :]
        return jnp.where(self.low, jnp.exp(jnp.where(self.low, gap, 0.0)), 0.0)


def unit(v):
    r = lax.rsqrt(jnp.sum(v * v, axis=-1, keepdims=True) + 1e-06)
    return v * r, r


def head_cols(h):
    return (
        slice(h * DK, (h + 1) * DK),
        slice(KD + h * DK, KD + (h + 1) * DK),
        slice(2 * KD + h * DV, 2 * KD + (h + 1) * DV),
        slice(QKV + h * DV, QKV + (h + 1) * DV),
    )


def mixer_fwd_kernel(len_ref, off_ref, pre_ref, taps_ref, gain_ref, dec_ref, mixed_ref, inv_ref, upd_ref, out_ref, low_ref):
    n = pre_ref.shape[0]
    bd = pre_ref[:, QKV + VD : QKV + VD + SMALL]
    blk = Block(len_ref, off_ref, bd, dec_ref[0:1], dec_ref[1:2])
    gain = gain_ref[...]
    lows, scores, rhs = [], [], []
    for h in range(H):
        cq, ck, cv, cg = head_cols(h)

        def conv_silu(cols):
            y = conv_sum(pre_ref[:, cols], taps_ref[:, cols], blk.keeps)
            return y * sigmoid(y)

        q = unit(conv_silu(cq))[0] * DK ** (-0.5)
        k = unit(conv_silu(ck))[0]
        v = conv_silu(cv)
        beta = blk.beta[:, h : h + 1]
        decay = blk.decay(h)
        lows.append(jnp.where(blk.strict, beta * decay * dot32(k, k, 1, 1), 0.0))
        scores.append(decay * dot32(q, k, 1, 1))
        rhs.append(beta * v)
    inv = []
    eye = jnp.where(blk.row == blk.col, 1.0, 0.0)
    pair = (blk.row // 2 == blk.col // 2) & (blk.row > blk.col)
    for h in range(H):
        inv.append(eye - jnp.where(pair, lows[h], 0.0))
    for h in range(H):
        inv_ref[:, h * n : (h + 1) * n] = inv[h]
        low_ref[:, h * n : (h + 1) * n] = lows[h]

    def level(k, _):
        outer = lax.shift_right_logical(blk.row, k + 1) == lax.shift_right_logical(blk.col, k + 1)
        part = outer & (lax.shift_right_logical(blk.row, k) > lax.shift_right_logical(blk.col, k))
        cols = [slice(h * n, (h + 1) * n) for h in range(H)]
        old = [inv_ref[:, c] for c in cols]
        mids = [dot32(jnp.where(part, low_ref[:, c], 0.0), t, 1, 0) for c, t in zip(cols, old)]
        for c, t, mid in zip(cols, old, mids):
            inv_ref[:, c] = t - dot32(t, mid, 1, 0)
        return 0

    lax.fori_loop(1, n.bit_length() - 1, level, 0)
    for h in range(H):
        _, _, _, cg = head_cols(h)
        cols = slice(h * DV, (h + 1) * DV)
        upd = dot32(inv_ref[:, h * n : (h + 1) * n], rhs[h], 1, 0)
        out = dot32(scores[h], upd, 1, 0)
        upd_ref[:, cols] = upd
        out_ref[:, cols] = out
        r = lax.rsqrt(jnp.mean(out * out, axis=-1, keepdims=True) + 1e-05)
        gate = pre_ref[:, cg]
        mixed_ref[:, cols] = (out * r * gain * (gate * sigmoid(gate))).astype(BF16)


def mixer_bwd_kernel(
    len_ref, off_ref, pre_ref, taps_ref, gain_ref, dec_ref, inv_ref, upd_ref, out_ref, dmix_ref,
    dpre_ref, dtaps_ref, dgain_ref, ddec_ref,
):
    n = pre_ref.shape[0]
    bd = pre_ref[:, QKV + VD : QKV + VD + SMALL]
    blk = Block(len_ref, off_ref, bd, dec_ref[0:1], dec_ref[1:2])
    gain = gain_ref[...]
    lane = lax.broadcasted_iota(jnp.int32, (n, SMALL), 1)
    d_gain = jnp.zeros((1, DV), F32)
    d_beta = jnp.zeros((n, SMALL), F32)
    d_cum = jnp.zeros((n, SMALL), F32)
    for h in range(H):
        cq, ck, cv, cg = head_cols(h)
        cols = slice(h * DV, (h + 1) * DV)
        out = out_ref[:, cols]
        gate = pre_ref[:, cg]
        d_mixed = dmix_ref[:, cols]
        r = lax.rsqrt(jnp.mean(out * out, axis=-1, keepdims=True) + 1e-05)
        sg = sigmoid(gate)
        silu_g = gate * sg
        unit_out = out * r
        d_normed = d_mixed * silu_g
        dpre_ref[:, cg] = (d_mixed * unit_out * gain * (sg * (1.0 + gate * (1.0 - sg)))).astype(BF16)
        d_gain = d_gain + jnp.sum(d_normed * unit_out, axis=0, keepdims=True)
        d_hat = d_normed * gain
        d_out = r * d_hat - out * (r * r * r) * jnp.mean(d_hat * out, axis=-1, keepdims=True)

        def conv_silu(cols_in):
            y = conv_sum(pre_ref[:, cols_in], taps_ref[:, cols_in], blk.keeps)
            s = sigmoid(y)
            return y * s, s * (1.0 + y * (1.0 - s))

        q_raw, q_slope = conv_silu(cq)
        k_raw, k_slope = conv_silu(ck)
        v, v_slope = conv_silu(cv)
        q_unit, q_r = unit(q_raw)
        k, k_r = unit(k_raw)
        scale = DK ** (-0.5)
        q = q_unit * scale
        beta = blk.beta[:, h : h + 1]
        decay = blk.decay(h)
        kk = dot32(k, k, 1, 1)
        qk = dot32(q, k, 1, 1)
        inv = inv_ref[:, h * n : (h + 1) * n]
        upd = upd_ref[:, cols]
        d_score = dot32(d_out, upd, 1, 1)
        d_upd = dot32(decay * qk, d_out, 0, 0)
        d_rhs = dot32(inv, d_upd, 0, 0)
        d_low = jnp.where(blk.strict, -dot32(d_rhs, upd, 1, 1), 0.0)
        dl = d_low * decay
        d_kk = dl * beta
        d_qk = d_score * decay
        d_beta_h = jnp.sum(dl * kk, axis=-1, keepdims=True) + jnp.sum(d_rhs * v, axis=-1, keepdims=True)
        d_gap = d_kk * kk + d_qk * qk
        d_cum_h = jnp.sum(d_gap - d_gap.T, axis=-1, keepdims=True)
        d_q = dot32(d_qk, k, 1, 0) * scale
        d_k = dot32(d_qk, q, 0, 0) + dot32(d_kk + d_kk.T, k, 1, 0)
        d_v = d_rhs * beta
        d_beta = d_beta + jnp.where(lane == h, d_beta_h, 0.0)
        d_cum = d_cum + jnp.where(lane == H + h, d_cum_h, 0.0)
        d_q_raw = q_r * d_q - q_raw * (q_r * q_r * q_r) * jnp.sum(d_q * q_raw, axis=-1, keepdims=True)
        d_k_raw = k_r * d_k - k_raw * (k_r * k_r * k_r) * jnp.sum(d_k * k_raw, axis=-1, keepdims=True)
        for c, d_y in ((cq, d_q_raw * q_slope), (ck, d_k_raw * k_slope), (cv, d_v * v_slope)):
            d_pre, d_taps = conv_grad(pre_ref[:, c], d_y, taps_ref[:, c], blk.keeps)
            dpre_ref[:, c] = d_pre.astype(BF16)
            for j in range(CONV):
                dtaps_ref[j : j + 1, c] = d_taps[j]
    d_log = dot32(blk.low_f, d_cum, 0, 0)
    d_shifted = d_log * (-blk.rate) * sigmoid(blk.shifted)
    d_bd = d_beta * blk.beta * (1.0 - blk.beta) + d_shifted
    dpre_ref[:, QKV + VD :] = d_bd.astype(BF16)
    dgain_ref[...] = d_gain
    ddec_ref[0:1] = jnp.sum(d_log * blk.logdecay, axis=0, keepdims=True)
    ddec_ref[1:2] = jnp.sum(d_shifted, axis=0, keepdims=True)


def vmem_specs(count):
    return [pl.BlockSpec(memory_space=pltpu.VMEM)] * count


def smem_specs(count):
    return [pl.BlockSpec(memory_space=pltpu.SMEM)] * count


def mixer_fwd(lengths, offsets, pre, taps, gain, dec):
    n = pre.shape[0]
    return pl.pallas_call(
        mixer_fwd_kernel,
        out_shape=(
            jax.ShapeDtypeStruct((n, VD), BF16),
            jax.ShapeDtypeStruct((n, H * n), F32),
            jax.ShapeDtypeStruct((n, VD), F32),
            jax.ShapeDtypeStruct((n, VD), F32),
        ),
        in_specs=smem_specs(2) + vmem_specs(4),
        out_specs=vmem_specs(4),
        scratch_shapes=[pltpu.VMEM((n, H * n), F32)],
        name="mixer_fwd",
    )(lengths, offsets, pre, taps, gain, dec)


def mixer_bwd(lengths, offsets, pre, taps, gain, dec, inv, upd, out, d_mixed):
    n = pre.shape[0]
    return pl.pallas_call(
        mixer_bwd_kernel,
        out_shape=(
            jax.ShapeDtypeStruct((n, QKV + VD + SMALL), BF16),
            jax.ShapeDtypeStruct((CONV, QKV), F32),
            jax.ShapeDtypeStruct((1, DV), F32),
            jax.ShapeDtypeStruct((2, SMALL), F32),
        ),
        in_specs=smem_specs(2) + vmem_specs(8),
        out_specs=vmem_specs(4),
        name="mixer_bwd",
    )(lengths, offsets, pre, taps, gain, dec, inv, upd, out, d_mixed)


class Links:
    def __init__(self, n_dev, x_bits, y_bits, z_bits):
        self.n = n_dev
        self.x, self.y, self.z = x_bits, y_bits, z_bits
        self.me = lax.axis_index("fsdp")
        self.chip_bits = sorted(x_bits + y_bits + z_bits, reverse=True)
        self.top = self.chip_bits[0]
        self.holder = self.bit(self.top) == self.bit(0)

    def bit(self, p):
        return lax.shift_right_logical(self.me, p) & 1

    def swap(self, array, p):
        return lax.ppermute(array, "fsdp", [(i, i ^ (1 << p)) for i in range(self.n)])

    def to_other_half(self, array, from_holder):
        pairs = [(i, i ^ (1 << self.top)) for i in range(self.n)]
        holds = lambda i: (i >> self.top) & 1 == i & 1
        return lax.ppermute(array, "fsdp", [(i, j) for i, j in pairs if holds(i) == from_holder])

    def in_order(self, p, mine, other, axis=0):
        low = self.bit(p) == 0
        return jnp.concatenate([jnp.where(low, mine, other), jnp.where(low, other, mine)], axis=axis)

    def spread(self, start, order):
        rows, held, shape = start
        for p in order:
            other = self.swap(rows, p)
            above = sum(1 for b in held if b > p)
            split = lambda a: a.reshape((2**above, 1, 2 ** (len(held) - above)) + shape)
            place = lax.broadcasted_iota(jnp.int32, (1, 2) + (1,) * (1 + len(shape)), 1)
            rows = jnp.where(place == self.bit(p), split(rows), split(other))
            held = held + [p]
            rows = rows.reshape((2 ** len(held),) + shape)
        return rows, held, shape

    def seed(self, rows):
        return rows[None], [], rows.shape

    def halve(self, array, bits, p):
        dim = bits.index(p)
        mine = self.bit(p)
        send = lax.dynamic_index_in_dim(array, 1 - mine, dim, keepdims=False)
        keep = lax.dynamic_index_in_dim(array, mine, dim, keepdims=False)
        return keep, self.swap(send, p), [b for b in bits if b != p]

    def first_half(self, left, right, bits, p):
        dim = bits.index(p)
        slots, rows = left.shape
        above, below = 2**dim, rows // 2 ** (dim + 1)
        split = left.T.reshape(above, 2, below, slots)
        mine = self.bit(p)
        pick = lambda b: lax.dynamic_index_in_dim(split, b, 1, keepdims=False).reshape(rows // 2, slots)
        return mm(pick(1 - mine), right).astype(BF16), pick(mine)

    def rest(self, sent, kept, right, bits, order):
        p = order[0]
        per = 2 * kept.shape[0] // 2 ** len(bits)
        got = self.swap(sent, p)
        total = got.astype(F32) + mm(kept, right)
        bits = [b for b in bits if b != p]
        for p in order[1:]:
            total = total.astype(BF16).reshape((2,) * len(bits) + (per, right.shape[1]))
            keep, got, bits = self.halve(total, bits, p)
            total = keep.astype(F32) + got.astype(F32)
        return total.reshape(per, right.shape[1])

    def grad_rows(self, left, right, bits, order):
        sent, kept = self.first_half(left, right, bits, order[0])
        return self.rest(sent, kept, right, bits, order)

    def small_sum(self, array):
        bits = self.chip_bits + [0]
        width = array.shape[1]
        array = array.reshape((2,) * len(bits) + (width // 128, 128))
        for p in [0] + self.z + self.x + self.y:
            keep, got, bits = self.halve(array, bits, p)
            array = keep + got
        return array.reshape(width)


def on_device(
    tokens, cotangent, lengths, offsets, norm_mix, w_query, w_key, w_value, w_gate, w_betadecay,
    conv_weight, out_gain, w_out, norm_ffn, w_ffgate, w_ffup, w_ffdown, decay_params, *, bits,
):
    slots, width = tokens.shape
    rows = w_query.shape[0]
    n_dev = width // rows
    ff = w_ffgate.shape[1]
    half_ff = ff // 2
    link = Links(n_dev, *bits)
    core = link.bit(0)
    first_core = core == 0
    chip_bits = link.chip_bits
    low_bits = chip_bits[1:]
    z_first = link.z[::-1]
    z_low = [p for p in z_first if p != link.top]

    choose = lambda a, b: jnp.where(first_core, a, b)

    def split_cores(array, axis):
        shape = array.shape[:axis] + (2, array.shape[axis] // 2) + array.shape[axis + 1 :]
        array = array.reshape(shape)
        pick = lambda b: lax.dynamic_index_in_dim(array, b, axis, keepdims=False)
        return pick(core), pick(1 - core)

    gain_col = jnp.concatenate([out_gain, jnp.zeros((rows - out_gain.shape[0],), BF16)])
    small_cols = jnp.concatenate(
        [w_betadecay, norm_mix[:, None], norm_ffn[:, None], conv_weight.reshape(rows, 2 * CONV), gain_col[:, None]],
        axis=1,
    )
    small_cols = jnp.pad(small_cols, ((0, 0), (0, SMALL - small_cols.shape[1])))
    full_mix = lax.all_gather(
        jnp.concatenate([w_query, w_key, w_value, w_gate, small_cols, w_out], axis=1), "fsdp", axis=0, tiled=True
    )
    gate_mine, gate_other = split_cores(w_ffgate, 1)
    up_mine, up_other = split_cores(w_ffup, 1)
    ffn_rows = link.in_order(
        0, jnp.concatenate([gate_mine, up_mine], axis=1), link.swap(jnp.concatenate([gate_other, up_other], axis=1), 0)
    )
    ffn_z, held, _ = link.spread(link.seed(ffn_rows), z_first)
    gate_z = (ffn_z[:, :, :half_ff], held, (2 * rows, half_ff))
    gate_w = link.spread(gate_z, link.x + link.y)[0].reshape(width, half_ff)
    up_z = (ffn_z[:, :, half_ff:], held, (2 * rows, half_ff))
    up_w = link.spread(up_z, link.y + link.x)[0].reshape(width, half_ff)
    down_rows = link.in_order(0, w_ffdown, link.swap(w_ffdown, 0))
    down_rows = jnp.where(link.holder, down_rows, link.to_other_half(down_rows, True))
    down_w = link.spread(link.seed(down_rows), link.x + link.y + z_low)[0].reshape(half_ff, width)

    proj = QKV + VD + SMALL
    small = full_mix[:, QKV + VD : proj].astype(F32)
    full_norm_mix = small[:, 2 * H]
    full_norm_ffn = small[:, 2 * H + 1]
    taps = small[:, 2 * H + 2 : 4 * H + 2].reshape(QKV, CONV).T
    gain = small[:, 4 * H + 2].reshape(n_dev, rows)[:, : out_gain.shape[0]].reshape(1, DV)
    full_in = full_mix[:, :proj]
    full_out = full_mix[:, proj:]
    dec = jnp.pad(decay_params, ((0, 0), (H, SMALL - 2 * H)))

    slot = jnp.arange(slots, dtype=jnp.int32)[:, None]
    valid = jnp.any((slot >= offsets) & (slot < offsets + lengths), axis=1)[:, None]
    top_grad = jnp.where(valid, cotangent.astype(F32), 0.0)
    top_narrow = top_grad.astype(BF16)
    top_both = jnp.concatenate([top_narrow, link.swap(top_narrow, 0)], axis=0)

    tokens_wide = tokens.astype(F32)
    r_mix = lax.rsqrt(jnp.mean(tokens_wide * tokens_wide, axis=-1, keepdims=True) + 1e-05)
    mix_input = (tokens_wide * r_mix * full_norm_mix).astype(BF16)
    pre = mm(mix_input, full_in)
    mixed, inv, upd, delta_out = mixer_fwd(lengths, offsets, pre, taps, gain, dec)
    residual = tokens_wide + mm(mixed, full_out)
    r_ffn = lax.rsqrt(jnp.mean(residual * residual, axis=-1, keepdims=True) + 1e-05)
    ffn_input = (residual * r_ffn * full_norm_ffn).astype(BF16)

    in_both = jnp.concatenate([ffn_input, link.swap(ffn_input, 0)], axis=0)
    up_gate = mm(in_both, gate_w)
    up_lin = mm(in_both, up_w)
    sig = jax.nn.sigmoid(up_gate)
    silu = up_gate * sig
    act = (silu * up_lin).astype(BF16)
    order_a = link.x + link.y + link.z
    order_b = link.y + link.x + link.z
    order_gate = link.y + link.z + link.x
    order_down = z_low[::-1] + link.x + link.y
    d_act = mm_t(top_both, down_w)
    d_gate = (d_act * up_lin * (sig * (1.0 + up_gate * (1.0 - sig)))).astype(BF16)
    d_up = (d_act * silu).astype(BF16)
    sent_down, kept_down = link.first_half(act, top_both, low_bits, order_down[0])
    sent_gate, kept_gate = link.first_half(in_both, d_gate, chip_bits, order_gate[0])
    sent_up, kept_up = link.first_half(in_both, d_up, chip_bits, order_a[0])

    def back_norm(values, r, gain_row, d_normed):
        d_hat = d_normed * gain_row
        d_gain = jnp.sum(d_normed * values * r, axis=0)
        mean = jnp.mean(d_hat * values, axis=-1, keepdims=True)
        return r * d_hat - values * (r * r * r) * mean, d_gain

    d_gate_late, d_up_late, _, _, _ = lax.optimization_barrier((d_gate, d_up, sent_down, sent_gate, sent_up))
    d_partial = mm_t(d_gate_late, gate_w) + mm_t(d_up_late, up_w)
    d_ffin = d_partial[:slots] + link.swap(d_partial[slots:], 0)
    d_res_norm, grad_norm_ffn = back_norm(residual, r_ffn, full_norm_ffn, d_ffin)
    d_residual = top_grad + d_res_norm
    d_res_narrow = d_residual.astype(BF16)

    def both(first, second):
        return jnp.concatenate([choose(first, second), link.swap(choose(second, first), 0)], axis=0)

    mix_both = jnp.concatenate([mix_input, link.swap(mix_input, 0)], axis=0)
    left_both = both(mix_input, mixed)
    d_mixed = mm_t(d_res_narrow, full_out)
    d_mixed, mix_both, left_both = lax.optimization_barrier((d_mixed, mix_both, left_both))
    d_pre, d_taps, d_gain, d_dec = mixer_bwd(
        lengths, offsets, pre, taps, gain, dec, inv, upd, delta_out, d_mixed
    )

    one_both = both(d_pre[:, : 2 * KD], d_pre[:, QKV : QKV + VD])
    two_both = both(d_pre[:, 2 * KD : QKV], d_res_narrow)
    sent_a, kept_a = link.first_half(mix_both, one_both, chip_bits, order_a[0])
    sent_b, kept_b = link.first_half(left_both, two_both, chip_bits, order_b[0])
    d_pre, d_taps, kept_down, kept_gate, kept_up, act_late, _, _ = lax.optimization_barrier(
        (d_pre, d_taps, kept_down, kept_gate, kept_up, act, sent_a, sent_b)
    )
    down_rows = link.rest(sent_down, kept_down, top_both, low_bits, order_down)
    grad_gate_rows = link.rest(sent_gate, kept_gate, d_gate, chip_bits, order_gate)
    grad_up_rows = link.rest(sent_up, kept_up, d_up, chip_bits, order_a)
    mix_a = link.rest(sent_a, kept_a, one_both, chip_bits, order_a)
    mix_b = link.rest(sent_b, kept_b, two_both, chip_bits, order_b)
    d_min = mm_t(d_pre, full_in)
    d_tok, grad_norm_mix = back_norm(tokens_wide, r_mix, full_norm_mix, d_min)
    input_grad = d_residual + d_tok
    partial = mm(act_late, down_w)
    final = residual + partial[:slots] + link.swap(partial[slots:], 0)
    output = jnp.where(valid, final, 0.0).astype(BF16)


    grad_bd = t_mm(mix_input, d_pre[:, QKV + VD :])[:, : 2 * H]
    d_dec_flat = d_dec[:, H : 2 * H].reshape(1, 2 * H)
    parts = [
        grad_bd.reshape(n_dev, -1),
        grad_norm_mix.reshape(n_dev, -1),
        grad_norm_ffn.reshape(n_dev, -1),
        d_taps.T.reshape(n_dev, -1),
        d_gain.reshape(n_dev, -1),
        jnp.broadcast_to(d_dec_flat, (n_dev, 2 * H)),
    ]
    packed = jnp.concatenate(parts, axis=1)
    pad = -packed.shape[1] % 1024
    summed = link.small_sum(jnp.pad(packed, ((0, 0), (0, pad))))
    pieces = []
    first = 0
    for part in parts:
        pieces.append(summed[first : first + part.shape[1]])
        first += part.shape[1]
    bd_rows, gain_mix, gain_ffn, conv_rows, gain_rows, dec_rows = pieces

    def settle(total):
        mine, other = split_cores(total, 0)
        other = link.swap(other, 0)
        return jnp.where(first_core, mine, other), jnp.where(first_core, other, mine)

    grad_ffgate = jnp.concatenate(settle(grad_gate_rows), axis=1)
    grad_ffup = jnp.concatenate(settle(grad_up_rows), axis=1)
    down_rows = down_rows + link.to_other_half(down_rows.astype(BF16), False).astype(F32)
    down_mine, down_other = split_cores(down_rows, 0)
    grad_ffdown = jnp.where(link.holder, down_mine, link.swap(down_other, 0))
    grad_qk, grad_gate = settle(mix_a)
    grad_value, grad_out = settle(mix_b)
    return (
        output,
        input_grad,
        gain_mix,
        grad_qk[:, :KD],
        grad_qk[:, KD:],
        grad_value,
        grad_gate,
        bd_rows.reshape(w_betadecay.shape),
        conv_rows.reshape(conv_weight.shape),
        gain_rows,
        grad_out,
        gain_ffn,
        grad_ffgate,
        grad_ffup,
        grad_ffdown,
        dec_rows.reshape(2, H),
    )


def axis_bits(mesh):
    coords = [d.coords for d in mesh.devices.flat]
    sizes = [1 + max(c[k] for c in coords) - min(c[k] for c in coords) for k in range(3)]
    spans, first = [], 1
    for size in sizes:
        count = size.bit_length() - 1
        spans.append(list(range(first, first + count)))
        first += count
    return spans


def solution(mesh):
    rows, vector = P("fsdp", None), P("fsdp")
    in_specs = (rows,) * 4 + (vector,) + (rows,) * 6 + (vector, rows, vector) + (rows,) * 3 + (P(),)
    out_specs = (rows,) * 2 + (vector,) + (rows,) * 6 + (vector, rows, vector) + (rows,) * 3 + (P(),)


    def body(*args):
        return on_device(*args, bits=axis_bits(mesh))

    return jax.shard_map(body, mesh=mesh, in_specs=in_specs, out_specs=out_specs, check_vma=False)
```

profile of v0, /device:TPU:0, one launch (start us, length us, event | category | flops | bytes accessed | tf_op | source)
XLA Modules:
  0.0 389.7 jit_solution(3743424295341272081)
XLA Ops:
  19.7 4.0 %collective-permute-start.8 = (bf16[1,64,2816]{2,1,0:T(8,128)(2,1)S(1)}, bf16[1,64,2816]{2,1,0:T(8,128)(2,1)S(1)}, u32[]{:S(2)}, u32[]{:S(2)}) collective-permute-start(bf16[1,64,2816]{2,1,0:T(8,128)(2,1)S(1)} %get-tuple-element.155), channel_id=1, source_target_pairs={{0,16},{1,17},{2,18},{3,19},{4,20},{5,21},{6,22},{7,23},{8,24},{9,... | collective-permute-start | bytes 1081352 | tf_op jit(solution)/shard_map/ppermute | solution.py:298
  25.8 24.6 %collective-permute-done.8 = bf16[1,64,2816]{2,1,0:T(8,128)(2,1)S(1)} collective-permute-done((bf16[1,64,2816]{2,1,0:T(8,128)(2,1)S(1)}, bf16[1,64,2816]{2,1,0:T(8,128)(2,1)S(1)}, u32[]{:S(2)}, u32[]{:S(2)}) %collective-permute-start.8) | collective-permute-done | bytes 360480 | tf_op jit(solution)/shard_map/ppermute | solution.py:298
  52.7 7.8 %collective-permute-done.3 = bf16[1,176,1024]{2,1,0:T(8,128)(2,1)S(1)} collective-permute-done((bf16[1,176,1024]{2,1,0:T(8,128)(2,1)S(1)}, bf16[1,176,1024]{2,1,0:T(8,128)(2,1)S(1)}, u32[]{:S(2)}, u32[]{:S(2)}) %collective-permute-start.3) | collective-permute-done | bytes 360480 | tf_op jit(solution)/shard_map/ppermute | solution.py:298
  62.5 18.0 %collective-permute-done.9 = bf16[2,64,2816]{2,1,0:T(8,128)(2,1)S(1)} collective-permute-done((bf16[2,64,2816]{2,1,0:T(8,128)(2,1)S(1)}, bf16[2,64,2816]{2,1,0:T(8,128)(2,1)S(1)}, u32[]{:S(2)}, u32[]{:S(2)}) %collective-permute-start.9) | collective-permute-done | bytes 720928 | tf_op jit(solution)/shard_map/ppermute | solution.py:298
  89.3 21.3 %collective-permute-done.12 = bf16[4,64,1408]{2,1,0:T(8,128)(2,1)} collective-permute-done((bf16[4,64,1408]{2,1,0:T(8,128)(2,1)S(1)}, bf16[4,64,1408]{2,1,0:T(8,128)(2,1)}, u32[]{:S(2)}, u32[]{:S(2)}) %collective-permute-start.12) | collective-permute-done | bytes 720928 | tf_op jit(solution)/shard_map/ppermute | solution.py:298
  110.5 2.5 bitcast_select_fusion.3
  115.7 2.7 bitcast_select_fusion.4
  119.3 14.4 %all-gather.2.cloned.1.call-done = bf16[1024,4224]{1,0:T(8,128)(2,1)} async-done(((bf16[32,4224]{1,0:T(8,128)(2,1)}), bf16[1024,4224]{1,0:T(8,128)(2,1)}) %all-gather.2.cloned.1.call-update) | async-done | bytes 8650768 | tf_op jit(solution)/shard_map/all_gather | solution.py:397
  136.4 5.2 %fusion.2.pre_ref = f32[128,3200]{1,0:T(8,128)} fusion(bf16[128,1024]{1,0:T(8,128)(2,1)} %fusion.26, bf16[1024,4224]{1,0:T(8,128)(2,1)} %all-gather.2.cloned.1.call-done), kind=kOutput, calls=%fused_computation.2 | convolution fusion | flops 838860800 | bytes 8454144 | tf_op jit(solution)/shard_map/dot_general | solution.py:28
  145.9 10.0 %mixer_fwd.1 = (bf16[128,1024]{1,0:T(8,128)(2,1)}, f32[128,512]{1,0:T(8,128)}, f32[128,1024]{1,0:T(8,128)}, f32[128,1024]{1,0:T(8,128)}) custom-call(s32[1,4]{1,0:T(1,128)} %len_ref.3, s32[1,4]{1,0:T(1,128)} %off_ref.3, f32[128,3200]{1,0:T(8,128)} %fusion.2.pre_ref, f32[4,2048]{1,0:T(4,128)} %bitcast.302, f32[1,256]{1,0:T(1,128)} %reshape.391.gain_ref, ...), custom_call_target="tpu_custom_call" | custom-call | tf_op jit(solution)/shard_map/mixer_fwd/pallas_call | solution.py:254
  159.9 3.4 bitcast_select_fusion.2
  178.8 3.3 constant_dynamic-slice_fusion.9
  184.0 5.1 %multiply_convert_fusion = (bf16[256,1408]{1,0:T(8,128)(2,1)}, bf16[256,1408]{1,0:T(8,128)(2,1)S(1)}, bf16[256,1408]{1,0:T(8,128)(2,1)S(1)}) fusion(f32[256,1408]{1,0:T(8,128)} %get-tuple-element.173, f32[256,1408]{1,0:T(8,128)} %copy-done.17, bf16[1408,1024]{1,0:T(8,128)(2,1)} %bitcast_select_fusion.2, bf16[128,1024]{1,0:T(8,128)(2,1)} %collective-permute-done, ...), kind=kOutput, calls=%fused_computation.38 | convolution fusion | flops 744652800 | bytes 8454144 | tf_op jit(solution)/shard_map/dot_general | solution.py:32
  193.3 2.7 convolution_convert_fusion.2
  206.0 3.2 fusion.4.dmix_ref
  209.4 11.3 %mixer_bwd.1 = (bf16[128,3200]{1,0:T(8,128)(2,1)}, f32[4,2048]{1,0:T(4,128)}, f32[1,256]{1,0:T(1,128)}, f32[2,128]{1,0:T(2,128)}) custom-call(s32[1,4]{1,0:T(1,128)} %len_ref.3, s32[1,4]{1,0:T(1,128)} %off_ref.3, f32[128,3200]{1,0:T(8,128)} %fusion.2.pre_ref, f32[4,2048]{1,0:T(4,128)} %bitcast.303, f32[1,256]{1,0:T(1,128)} %reshape.391.gain_ref, ...), custom_call_target="tpu_custom_call" | custom-call | tf_op jit(solution)/shard_map/mixer_bwd/pallas_call | solution.py:271
  234.5 6.2 %fusion.32 = (f32[1024]{0:T(1024)S(1)}, f32[128]{0:T(128)S(1)}, f32[128,1024]{1,0:T(8,128)}) fusion(bf16[128,1024]{1,0:T(8,128)(2,1)S(1)} %copy-done.6, f32[128]{0:T(128)S(1)} %get-tuple-element.167, f32[1024]{0:T(1024)S(1)} %get-tuple-element.124, bf16[128,3200]{1,0:T(8,128)(2,1)} %get-tuple-element.47, bf16[1024,4224]{1,0:T(8,128)(2,1)} %all-gather.2.cloned.1.call-done), kind=kOutput, calls=%fused_computation.75 | convolution fusion | flops 839777152 | bytes 8168448 | tf_op jit(solution)/shard_map/dot_general | solution.py:32
  243.3 5.6 %collective-permute-start.21 = (f32[2,2,2,8,128]{4,3,2,1,0:T(8,128)S(1)}, f32[2,2,2,8,128]{4,3,2,1,0:T(8,128)S(1)}, u32[]{:S(2)}, u32[]{:S(2)}) collective-permute-start(f32[2,2,2,8,128]{4,3,2,1,0:T(8,128)S(1)} %dynamic-slice_bitcast_fusion.21), channel_id=1, source_target_pairs={{0,8},{1,9},{2,10},{3,11},{4,12},{5,13},{6,14},{7,15},{8,0},{9,1},... | collective-permute-start | bytes 98312 | tf_op jit(solution)/shard_map/ppermute | solution.py:298
  251.5 3.7 collective-permute-start.22
  255.3 2.8 fusion.74
  259.0 22.8 %collective-permute-done.22 = f32[2,2,8,128]{3,2,1,0:T(8,128)S(1)} collective-permute-done((f32[2,2,8,128]{3,2,1,0:T(8,128)S(1)}, f32[2,2,8,128]{3,2,1,0:T(8,128)S(1)}, u32[]{:S(2)}, u32[]{:S(2)}) %collective-permute-start.22) | collective-permute-done | bytes 16416 | tf_op jit(solution)/shard_map/ppermute | solution.py:298
  298.9 4.2 %collective-permute-start.36 = (bf16[2,2,64,1408]{3,2,1,0:T(8,128)(2,1)S(1)}, bf16[2,2,64,1408]{3,2,1,0:T(8,128)(2,1)S(1)}, u32[]{:S(2)}, u32[]{:S(2)}) collective-permute-start(bf16[2,2,64,1408]{3,2,1,0:T(8,128)(2,1)S(1)} %dynamic-slice_bitcast_fusion.2), channel_id=1, source_target_pairs={{0,8},{1,9},{2,10},{3,11},{4,12},{5,13},{6,14},{7,15},{8,0},{9,1},... | collective-permute-start | bytes 2162696 | tf_op jit(solution)/shard_map/ppermute | solution.py:298
  309.1 6.4 %collective-permute-done.25 = bf16[512,1024]{1,0:T(8,128)(2,1)} collective-permute-done((bf16[512,1024]{1,0:T(8,128)(2,1)}, bf16[512,1024]{1,0:T(8,128)(2,1)}, u32[]{:S(2)}, u32[]{:S(2)}) %collective-permute-start.25) | collective-permute-done | bytes 1048608 | tf_op jit(solution)/shard_map/ppermute | solution.py:298
  321.3 3.4 collective-permute-start.37
  324.7 10.9 %collective-permute-done.41 = bf16[2,2,64,1408]{3,2,1,0:T(8,128)(2,1)S(1)} collective-permute-done((bf16[2,2,64,1408]{3,2,1,0:T(8,128)(2,1)S(1)}, bf16[2,2,64,1408]{3,2,1,0:T(8,128)(2,1)S(1)}, u32[]{:S(2)}, u32[]{:S(2)}) %collective-permute-start.41) | collective-permute-done | bytes 720928 | tf_op jit(solution)/shard_map/ppermute | solution.py:298
  335.9 4.2 %collective-permute-start.42 = (bf16[2,64,1408]{2,1,0:T(8,128)(2,1)S(1)}, bf16[2,64,1408]{2,1,0:T(8,128)(2,1)S(1)}, u32[]{:S(2)}, u32[]{:S(2)}) collective-permute-start(bf16[2,64,1408]{2,1,0:T(8,128)(2,1)S(1)} %dynamic-slice_bitcast_fusion.7), channel_id=1, source_target_pairs={{0,8},{1,9},{2,10},{3,11},{4,12},{5,13},{6,14},{7,15},{8,0},{9,1},... | collective-permute-start | bytes 1081352 | tf_op jit(solution)/shard_map/ppermute | solution.py:298
  341.2 5.3 %collective-permute-done.26 = bf16[2,2,64,1024]{3,2,1,0:T(8,128)(2,1)S(1)} collective-permute-done((bf16[2,2,64,1024]{3,2,1,0:T(8,128)(2,1)S(1)}, bf16[2,2,64,1024]{3,2,1,0:T(8,128)(2,1)S(1)}, u32[]{:S(2)}, u32[]{:S(2)}) %collective-permute-start.26) | collective-permute-done | bytes 524320 | tf_op jit(solution)/shard_map/ppermute | solution.py:298
  346.7 3.8 collective-permute-start.27
  354.1 3.6 collective-permute-done.27
  359.0 4.6 %collective-permute-done.32 = bf16[2,64,1024]{2,1,0:T(8,128)(2,1)S(1)} collective-permute-done((bf16[2,64,1024]{2,1,0:T(8,128)(2,1)S(1)}, bf16[2,64,1024]{2,1,0:T(8,128)(2,1)S(1)}, u32[]{:S(2)}, u32[]{:S(2)}) %collective-permute-start.32) | collective-permute-done | bytes 262176 | tf_op jit(solution)/shard_map/ppermute | solution.py:298
  364.0 2.6 collective-permute-done.43
  366.8 9.1 %collective-permute-done.28 = bf16[64,1024]{1,0:T(8,128)(2,1)S(1)} collective-permute-done((bf16[64,1024]{1,0:T(8,128)(2,1)S(1)}, bf16[64,1024]{1,0:T(8,128)(2,1)S(1)}, u32[]{:S(2)}, u32[]{:S(2)}) %collective-permute-start.28) | collective-permute-done | bytes 131104 | tf_op jit(solution)/shard_map/ppermute | solution.py:298
  (352 shorter events, 135.8 us)
Async XLA Ops:
  7.2 126.5 %all-gather.2.cloned.1.call-start = ((), (), s32[]{:S(2)}) async-start(), calls=%async_computation | async-start | bytes 8921088 | tf_op jit(solution)/shard_map/all_gather | solution.py:397
  19.7 30.7 %collective-permute-start.8 = (bf16[1,64,2816]{2,1,0:T(8,128)(2,1)S(1)}, bf16[1,64,2816]{2,1,0:T(8,128)(2,1)S(1)}, u32[]{:S(2)}, u32[]{:S(2)}) collective-permute-start(bf16[1,64,2816]{2,1,0:T(8,128)(2,1)S(1)} %get-tuple-element.155), channel_id=1, source_target_pairs={{0,16},{1,17},{2,18},{3,19},{4,20},{5,21},{6,22},{7,23},{8,24},{9,... | collective-permute-start | bytes 1081352 | tf_op jit(solution)/shard_map/ppermute | solution.py:298
  23.8 27.0 %collective-permute-start.2 = (bf16[176,1024]{1,0:T(8,128)(2,1)S(1)}, bf16[176,1024]{1,0:T(8,128)(2,1)S(1)}, u32[]{:S(2)}, u32[]{:S(2)}) collective-permute-start(bf16[176,1024]{1,0:T(8,128)(2,1)S(1)} %pad_maximum_fusion.6), channel_id=1, source_target_pairs={{0,16},{2,18},{4,20},{6,22},{8,24},{10,26},{12,28},{14,30},{17,1},... | collective-permute-start | bytes 1081352 | tf_op jit(solution)/shard_map/ppermute | solution.py:303
  50.5 30.0 %collective-permute-start.9 = (bf16[2,64,2816]{2,1,0:T(8,128)(2,1)S(1)}, bf16[2,64,2816]{2,1,0:T(8,128)(2,1)S(1)}, u32[]{:S(2)}, u32[]{:S(2)}) collective-permute-start(bf16[2,64,2816]{2,1,0:T(8,128)(2,1)S(1)} %broadcast_select_fusion.1), channel_id=1, source_target_pairs={{0,8},{1,9},{2,10},{3,11},{4,12},{5,13},{6,14},{7,15},{8,0},{9,1},... | collective-permute-start | bytes 2162696 | tf_op jit(solution)/shard_map/ppermute | solution.py:298
  60.7 27.0 %collective-permute-start.4 = (bf16[2,176,1024]{2,1,0:T(8,128)(2,1)S(1)}, bf16[2,176,1024]{2,1,0:T(8,128)(2,1)}, u32[]{:S(2)}, u32[]{:S(2)}) collective-permute-start(bf16[2,176,1024]{2,1,0:T(8,128)(2,1)S(1)} %broadcast_select_fusion.2), channel_id=1, source_target_pairs={{0,4},{1,5},{2,6},{3,7},{4,0},{5,1},{6,2},{7,3},{8,12},{9,13},{10,... | collective-permute-start | bytes 2162696 | tf_op jit(solution)/shard_map/ppermute | solution.py:298
  81.8 28.8 %collective-permute-start.12 = (bf16[4,64,1408]{2,1,0:T(8,128)(2,1)S(1)}, bf16[4,64,1408]{2,1,0:T(8,128)(2,1)}, u32[]{:S(2)}, u32[]{:S(2)}) collective-permute-start(bf16[4,64,1408]{2,1,0:T(8,128)(2,1)S(1)} %get-tuple-element.129), channel_id=1, source_target_pairs={{0,2},{1,3},{2,0},{3,1},{4,6},{5,7},{6,4},{7,5},{8,10},{9,11},{10,... | collective-permute-start | bytes 2162696 | tf_op jit(solution)/shard_map/ppermute | solution.py:298
  83.6 32.1 %collective-permute-start.10 = (bf16[4,64,1408]{2,1,0:T(8,128)(2,1)}, bf16[4,64,1408]{2,1,0:T(8,128)(2,1)}, u32[]{:S(2)}, u32[]{:S(2)}) collective-permute-start(bf16[4,64,1408]{2,1,0:T(8,128)(2,1)} %get-tuple-element.128), channel_id=1, source_target_pairs={{0,4},{1,5},{2,6},{3,7},{4,0},{5,1},{6,2},{7,3},{8,12},{9,13},{10,... | collective-permute-start | bytes 2162696 | tf_op jit(solution)/shard_map/ppermute | solution.py:298
  86.0 98.0 %collective-permute-start = (bf16[128,1024]{1,0:T(8,128)(2,1)}, bf16[128,1024]{1,0:T(8,128)(2,1)}, u32[]{:S(2)}, u32[]{:S(2)}) collective-permute-start(bf16[128,1024]{1,0:T(8,128)(2,1)} %fusion.38), channel_id=1, source_target_pairs={{0,1},{1,0},{2,3},{3,2},{4,5},{5,4},{6,7},{7,6},{8,9},{9,8},{10,11... | collective-permute-start | bytes 786440 | tf_op jit(solution)/shard_map/ppermute | solution.py:298
  89.2 70.7 %collective-permute-start.5 = (bf16[4,176,1024]{2,1,0:T(8,128)(2,1)S(1)}, bf16[4,176,1024]{2,1,0:T(8,128)(2,1)}, u32[]{:S(2)}, u32[]{:S(2)}) collective-permute-start(bf16[4,176,1024]{2,1,0:T(8,128)(2,1)S(1)} %bitcast_select_fusion.6), channel_id=1, source_target_pairs={{0,8},{1,9},{2,10},{3,11},{4,12},{5,13},{6,14},{7,15},{8,0},{9,1},... | collective-permute-start | bytes 4325384 | tf_op jit(solution)/shard_map/ppermute | solution.py:298
  113.0 50.2 %collective-permute-start.13 = (bf16[8,64,1408]{2,1,0:T(8,128)(2,1)}, bf16[8,64,1408]{2,1,0:T(8,128)(2,1)}, u32[]{:S(2)}, u32[]{:S(2)}) collective-permute-start(bf16[8,64,1408]{2,1,0:T(8,128)(2,1)} %bitcast_select_fusion.3), channel_id=1, source_target_pairs={{0,4},{1,5},{2,6},{3,7},{4,0},{5,1},{6,2},{7,3},{8,12},{9,13},{10,... | collective-permute-start | bytes 4325384 | tf_op jit(solution)/shard_map/ppermute | solution.py:298
  118.3 46.8 %collective-permute-start.11 = (bf16[8,64,1408]{2,1,0:T(8,128)(2,1)}, bf16[8,64,1408]{2,1,0:T(8,128)(2,1)}, u32[]{:S(2)}, u32[]{:S(2)}) collective-permute-start(bf16[8,64,1408]{2,1,0:T(8,128)(2,1)} %bitcast_select_fusion.4), channel_id=1, source_target_pairs={{0,2},{1,3},{2,0},{3,1},{4,6},{5,7},{6,4},{7,5},{8,10},{9,11},{10,... | collective-permute-start | bytes 4325384 | tf_op jit(solution)/shard_map/ppermute | solution.py:298
  167.3 35.4 %collective-permute-start.15 = (bf16[128,1024]{1,0:T(8,128)(2,1)}, bf16[128,1024]{1,0:T(8,128)(2,1)}, u32[]{:S(2)}, u32[]{:S(2)}) collective-permute-start(bf16[128,1024]{1,0:T(8,128)(2,1)} %fusion.26), channel_id=1, source_target_pairs={{0,1},{1,0},{2,3},{3,2},{4,5},{5,4},{6,7},{7,6},{8,9},{9,8},{10,11... | collective-permute-start | bytes 786440 | tf_op jit(solution)/shard_map/ppermute | solution.py:298
  248.9 48.0 %collective-permute-start.35 = (bf16[512,1408]{1,0:T(8,128)(2,1)}, bf16[512,1408]{1,0:T(8,128)(2,1)}, u32[]{:S(2)}, u32[]{:S(2)}) collective-permute-start(bf16[512,1408]{1,0:T(8,128)(2,1)} %convolution_convert_fusion.1), channel_id=1, source_target_pairs={{0,4},{1,5},{2,6},{3,7},{4,0},{5,1},{6,2},{7,3},{8,12},{9,13},{10,... | collective-permute-start | bytes 4325384 | tf_op jit(solution)/shard_map/ppermute | solution.py:298
  250.2 52.9 %collective-permute-start.40 = (bf16[512,1408]{1,0:T(8,128)(2,1)}, bf16[512,1408]{1,0:T(8,128)(2,1)}, u32[]{:S(2)}, u32[]{:S(2)}) collective-permute-start(bf16[512,1408]{1,0:T(8,128)(2,1)} %convolution_convert_fusion), channel_id=1, source_target_pairs={{0,2},{1,3},{2,0},{3,1},{4,6},{5,7},{6,4},{7,5},{8,10},{9,11},{10,... | collective-permute-start | bytes 4325384 | tf_op jit(solution)/shard_map/ppermute | solution.py:298
  250.3 56.2 %collective-permute-start.45 = (bf16[704,1024]{1,0:T(8,128)(2,1)}, bf16[704,1024]{1,0:T(8,128)(2,1)}, u32[]{:S(2)}, u32[]{:S(2)}) collective-permute-start(bf16[704,1024]{1,0:T(8,128)(2,1)} %convolution_convert_fusion.2), channel_id=1, source_target_pairs={{0,8},{1,9},{2,10},{3,11},{4,12},{5,13},{6,14},{7,15},{8,0},{9,1},... | collective-permute-start | bytes 4325384 | tf_op jit(solution)/shard_map/ppermute | solution.py:298
  251.5 30.3 %collective-permute-start.22 = (f32[2,2,8,128]{3,2,1,0:T(8,128)S(1)}, f32[2,2,8,128]{3,2,1,0:T(8,128)S(1)}, u32[]{:S(2)}, u32[]{:S(2)}) collective-permute-start(f32[2,2,8,128]{3,2,1,0:T(8,128)S(1)} %dynamic-slice_bitcast_fusion.22), channel_id=1, source_target_pairs={{0,16},{1,17},{2,18},{3,19},{4,20},{5,21},{6,22},{7,23},{8,24},{9,... | collective-permute-start | bytes 49160 | tf_op jit(solution)/shard_map/ppermute | solution.py:298
  259.0 35.1 %collective-permute-start.19 = (f32[128,1024]{1,0:T(8,128)}, f32[128,1024]{1,0:T(8,128)}, u32[]{:S(2)}, u32[]{:S(2)}) collective-permute-start(f32[128,1024]{1,0:T(8,128)} %slice.133), channel_id=1, source_target_pairs={{0,1},{1,0},{2,3},{3,2},{4,5},{5,4},{6,7},{7,6},{8,9},{9,8},{10,11... | collective-permute-start | bytes 1572872 | tf_op jit(solution)/shard_map/ppermute | solution.py:298
  289.1 26.4 %collective-permute-start.25 = (bf16[512,1024]{1,0:T(8,128)(2,1)}, bf16[512,1024]{1,0:T(8,128)(2,1)}, u32[]{:S(2)}, u32[]{:S(2)}) collective-permute-start(bf16[512,1024]{1,0:T(8,128)(2,1)} %convolution_convert_fusion.4), channel_id=1, source_target_pairs={{0,2},{1,3},{2,0},{3,1},{4,6},{5,7},{6,4},{7,5},{8,10},{9,11},{10,... | collective-permute-start | bytes 3145736 | tf_op jit(solution)/shard_map/ppermute | solution.py:298
  294.1 26.0 %collective-permute-start.30 = (bf16[512,1024]{1,0:T(8,128)(2,1)S(1)}, bf16[512,1024]{1,0:T(8,128)(2,1)S(1)}, u32[]{:S(2)}, u32[]{:S(2)}) collective-permute-start(bf16[512,1024]{1,0:T(8,128)(2,1)S(1)} %copy-done.19), channel_id=1, source_target_pairs={{0,4},{1,5},{2,6},{3,7},{4,0},{5,1},{6,2},{7,3},{8,12},{9,13},{10,... | collective-permute-start | bytes 3145736 | tf_op jit(solution)/shard_map/ppermute | solution.py:298
  298.9 22.2 %collective-permute-start.36 = (bf16[2,2,64,1408]{3,2,1,0:T(8,128)(2,1)S(1)}, bf16[2,2,64,1408]{3,2,1,0:T(8,128)(2,1)S(1)}, u32[]{:S(2)}, u32[]{:S(2)}) collective-permute-start(bf16[2,2,64,1408]{3,2,1,0:T(8,128)(2,1)S(1)} %dynamic-slice_bitcast_fusion.2), channel_id=1, source_target_pairs={{0,8},{1,9},{2,10},{3,11},{4,12},{5,13},{6,14},{7,15},{8,0},{9,1},... | collective-permute-start | bytes 2162696 | tf_op jit(solution)/shard_map/ppermute | solution.py:298
  305.1 30.5 %collective-permute-start.41 = (bf16[2,2,64,1408]{3,2,1,0:T(8,128)(2,1)S(1)}, bf16[2,2,64,1408]{3,2,1,0:T(8,128)(2,1)S(1)}, u32[]{:S(2)}, u32[]{:S(2)}) collective-permute-start(bf16[2,2,64,1408]{3,2,1,0:T(8,128)(2,1)S(1)} %dynamic-slice_bitcast_fusion.1), channel_id=1, source_target_pairs={{0,4},{1,5},{2,6},{3,7},{4,0},{5,1},{6,2},{7,3},{8,12},{9,13},{10,... | collective-permute-start | bytes 2162696 | tf_op jit(solution)/shard_map/ppermute | solution.py:298
  308.7 31.4 %collective-permute-start.46 = (bf16[2,176,1024]{2,1,0:T(8,128)(2,1)S(1)}, bf16[2,176,1024]{2,1,0:T(8,128)(2,1)S(1)}, u32[]{:S(2)}, u32[]{:S(2)}) collective-permute-start(bf16[2,176,1024]{2,1,0:T(8,128)(2,1)S(1)} %dynamic-slice_bitcast_fusion), channel_id=1, source_target_pairs={{0,2},{1,3},{2,0},{3,1},{4,6},{5,7},{6,4},{7,5},{8,10},{9,11},{10,... | collective-permute-start | bytes 2162696 | tf_op jit(solution)/shard_map/ppermute | solution.py:298
  317.3 29.1 %collective-permute-start.26 = (bf16[2,2,64,1024]{3,2,1,0:T(8,128)(2,1)S(1)}, bf16[2,2,64,1024]{3,2,1,0:T(8,128)(2,1)S(1)}, u32[]{:S(2)}, u32[]{:S(2)}) collective-permute-start(bf16[2,2,64,1024]{3,2,1,0:T(8,128)(2,1)S(1)} %dynamic-slice_bitcast_fusion.4), channel_id=1, source_target_pairs={{0,4},{1,5},{2,6},{3,7},{4,0},{5,1},{6,2},{7,3},{8,12},{9,13},{10,... | collective-permute-start | bytes 1572872 | tf_op jit(solution)/shard_map/ppermute | solution.py:298
  320.7 29.8 %collective-permute-start.31 = (bf16[2,2,64,1024]{3,2,1,0:T(8,128)(2,1)S(1)}, bf16[2,2,64,1024]{3,2,1,0:T(8,128)(2,1)S(1)}, u32[]{:S(2)}, u32[]{:S(2)}) collective-permute-start(bf16[2,2,64,1024]{3,2,1,0:T(8,128)(2,1)S(1)} %dynamic-slice_bitcast_fusion.3), channel_id=1, source_target_pairs={{0,2},{1,3},{2,0},{3,1},{4,6},{5,7},{6,4},{7,5},{8,10},{9,11},{10,... | collective-permute-start | bytes 1572872 | tf_op jit(solution)/shard_map/ppermute | solution.py:298
  321.3 29.5 %collective-permute-start.37 = (bf16[2,64,1408]{2,1,0:T(8,128)(2,1)S(1)}, bf16[2,64,1408]{2,1,0:T(8,128)(2,1)S(1)}, u32[]{:S(2)}, u32[]{:S(2)}) collective-permute-start(bf16[2,64,1408]{2,1,0:T(8,128)(2,1)S(1)} %dynamic-slice_bitcast_fusion.8), channel_id=1, source_target_pairs={{0,16},{1,17},{2,18},{3,19},{4,20},{5,21},{6,22},{7,23},{8,24},{9,... | collective-permute-start | bytes 1081352 | tf_op jit(solution)/shard_map/ppermute | solution.py:298
  335.9 15.4 %collective-permute-start.42 = (bf16[2,64,1408]{2,1,0:T(8,128)(2,1)S(1)}, bf16[2,64,1408]{2,1,0:T(8,128)(2,1)S(1)}, u32[]{:S(2)}, u32[]{:S(2)}) collective-permute-start(bf16[2,64,1408]{2,1,0:T(8,128)(2,1)S(1)} %dynamic-slice_bitcast_fusion.7), channel_id=1, source_target_pairs={{0,8},{1,9},{2,10},{3,11},{4,12},{5,13},{6,14},{7,15},{8,0},{9,1},... | collective-permute-start | bytes 1081352 | tf_op jit(solution)/shard_map/ppermute | solution.py:298
  351.4 15.2 %collective-permute-start.43 = (bf16[64,1408]{1,0:T(8,128)(2,1)S(1)}, bf16[64,1408]{1,0:T(8,128)(2,1)S(1)}, u32[]{:S(2)}, u32[]{:S(2)}) collective-permute-start(bf16[64,1408]{1,0:T(8,128)(2,1)S(1)} %dynamic-slice_bitcast_fusion.13), channel_id=1, source_target_pairs={{0,16},{1,17},{2,18},{3,19},{4,20},{5,21},{6,22},{7,23},{8,24},{9,... | collective-permute-start | bytes 540680 | tf_op jit(solution)/shard_map/ppermute | solution.py:298
  352.8 24.6 %collective-permute-start.48 = (bf16[176,1024]{1,0:T(8,128)(2,1)S(1)}, bf16[176,1024]{1,0:T(8,128)(2,1)S(1)}, u32[]{:S(2)}, u32[]{:S(2)}) collective-permute-start(bf16[176,1024]{1,0:T(8,128)(2,1)S(1)} %fusion.23), channel_id=1, source_target_pairs={{1,17},{3,19},{5,21},{7,23},{9,25},{11,27},{13,29},{15,31},{16,0},... | collective-permute-start | bytes 1081352 | tf_op jit(solution)/shard_map/ppermute | solution.py:303
  357.8 18.1 %collective-permute-start.28 = (bf16[64,1024]{1,0:T(8,128)(2,1)S(1)}, bf16[64,1024]{1,0:T(8,128)(2,1)S(1)}, u32[]{:S(2)}, u32[]{:S(2)}) collective-permute-start(bf16[64,1024]{1,0:T(8,128)(2,1)S(1)} %dynamic-slice_bitcast_fusion.19), channel_id=1, source_target_pairs={{0,16},{1,17},{2,18},{3,19},{4,20},{5,21},{6,22},{7,23},{8,24},{9,... | collective-permute-start | bytes 393224 | tf_op jit(solution)/shard_map/ppermute | solution.py:298
  363.8 13.5 %collective-permute-start.33 = (bf16[64,1024]{1,0:T(8,128)(2,1)S(1)}, bf16[64,1024]{1,0:T(8,128)(2,1)S(1)}, u32[]{:S(2)}, u32[]{:S(2)}) collective-permute-start(bf16[64,1024]{1,0:T(8,128)(2,1)S(1)} %dynamic-slice_bitcast_fusion.17), channel_id=1, source_target_pairs={{0,16},{1,17},{2,18},{3,19},{4,20},{5,21},{6,22},{7,23},{8,24},{9,... | collective-permute-start | bytes 393224 | tf_op jit(solution)/shard_map/ppermute | solution.py:298
  363.9 14.3 %collective-permute-start.39 = (f32[32,1408]{1,0:T(8,128)S(1)}, f32[32,1408]{1,0:T(8,128)S(1)}, u32[]{:S(2)}, u32[]{:S(2)}) collective-permute-start(f32[32,1408]{1,0:T(8,128)S(1)} %dynamic-slice_bitcast_fusion.14), channel_id=1, source_target_pairs={{0,1},{1,0},{2,3},{3,2},{4,5},{5,4},{6,7},{7,6},{8,9},{9,8},{10,11... | collective-permute-start | bytes 540680 | tf_op jit(solution)/shard_map/ppermute | solution.py:298
  366.7 13.7 %collective-permute-start.44 = (f32[32,1408]{1,0:T(8,128)S(1)}, f32[32,1408]{1,0:T(8,128)S(1)}, u32[]{:S(2)}, u32[]{:S(2)}) collective-permute-start(f32[32,1408]{1,0:T(8,128)S(1)} %dynamic-slice_bitcast_fusion.12), channel_id=1, source_target_pairs={{0,1},{1,0},{2,3},{3,2},{4,5},{5,4},{6,7},{7,6},{8,9},{9,8},{10,11... | collective-permute-start | bytes 540680 | tf_op jit(solution)/shard_map/ppermute | solution.py:298
  (61 other events, 456.0 us)
Sparse Core Ops, SparseCore 0:
  16.2 117.4 all-gather.1
where the time goes:
time: 397 us; the launch traced here: 390 us
  waiting for transfers between devices  161 us (41%)
  starting transfers between devices  58.9 us (15%)
  matrix products  49.5 us (12%)
  local copies, waits for them, and re-layouts  49.4 us (12%)
  other arithmetic  34 us (9%)
  Pallas kernels  21.2 us (5%)
  between operations  15.4 us (4%)
    ppermute x48, waiting for transfers between devices, swap(): return lax.ppermute(array, 'fsdp', [(i, i ^ 1 << p) for i in range(self.n)])  147 us
    ppermute x48, starting transfers between devices, swap(): return lax.ppermute(array, 'fsdp', [(i, i ^ 1 << p) for i in range(self.n)])  55.6 us
    dot_general x15, matrix products, mm(): return jnp.dot(a, b, preferred_element_type=F32)  31.8 us
    dot_general x5, matrix products, mm_t(): lax.dot_general(a, b, (((1,), (1,)), ((), ())), preferred_element_type=F32)  16.5 us
    select_n x10, other arithmetic, spread(): rows = jnp.where(place == self.bit(p), split(rows), split(other))  15.9 us
    unnamed x103, local copies, waits for them, and re-layouts  14.8 us
    all_gather x1, waiting for transfers between devices, on_device(): lax.all_gather(jnp.concatenate([w_query, w_key, w_value, w_gate, small_co...  14.4 us
    pallas_call x1, Pallas kernels, mixer_bwd(): pl.pallas_call(mixer_bwd_kernel, out_shape=(jax.ShapeDtypeStruct((n, QKV...  11.3 us
  transfers between devices with their start and end apart: 51, of which 20 were waited for; matrix products, arithmetic and copies ran while one was open for 27% of the time, Pallas kernels for 3%

commit v1 on v0

--- a/solution.py
+++ b/solution.py
@@ -328,11 +328,11 @@
         keep = lax.dynamic_index_in_dim(array, mine, dim, keepdims=False)
         return keep, self.swap(send, p), [b for b in bits if b != p]
 
-    def first_half(self, left, right, bits, p):
+    def first_half(self, left_t, right, bits, p):
         dim = bits.index(p)
-        slots, rows = left.shape
+        rows, slots = left_t.shape
         above, below = 2**dim, rows // 2 ** (dim + 1)
-        split = left.T.reshape(above, 2, below, slots)
+        split = left_t.reshape(above, 2, below, slots)
         mine = self.bit(p)
         pick = lambda b: lax.dynamic_index_in_dim(split, b, 1, keepdims=False).reshape(rows // 2, slots)
         return mm(pick(1 - mine), right).astype(BF16), pick(mine)
@@ -449,9 +449,10 @@
     d_act = mm_t(top_both, down_w)
     d_gate = (d_act * up_lin * (sig * (1.0 + up_gate * (1.0 - sig)))).astype(BF16)
     d_up = (d_act * silu).astype(BF16)
-    sent_down, kept_down = link.first_half(act, top_both, low_bits, order_down[0])
-    sent_gate, kept_gate = link.first_half(in_both, d_gate, chip_bits, order_gate[0])
-    sent_up, kept_up = link.first_half(in_both, d_up, chip_bits, order_a[0])
+    in_both_t, act_t = lax.optimization_barrier((in_both.T, act.T))
+    sent_down, kept_down = link.first_half(act_t, top_both, low_bits, order_down[0])
+    sent_gate, kept_gate = link.first_half(in_both_t, d_gate, chip_bits, order_gate[0])
+    sent_up, kept_up = link.first_half(in_both_t, d_up, chip_bits, order_a[0])
 
     def back_norm(values, r, gain_row, d_normed):
         d_hat = d_normed * gain_row
@@ -472,15 +473,15 @@
     mix_both = jnp.concatenate([mix_input, link.swap(mix_input, 0)], axis=0)
     left_both = both(mix_input, mixed)
     d_mixed = mm_t(d_res_narrow, full_out)
-    d_mixed, mix_both, left_both = lax.optimization_barrier((d_mixed, mix_both, left_both))
+    d_mixed, mix_both_t, left_both_t = lax.optimization_barrier((d_mixed, mix_both.T, left_both.T))
     d_pre, d_taps, d_gain, d_dec = mixer_bwd(
         lengths, offsets, pre, taps, gain, dec, inv, upd, delta_out, d_mixed
     )
 
     one_both = both(d_pre[:, : 2 * KD], d_pre[:, QKV : QKV + VD])
     two_both = both(d_pre[:, 2 * KD : QKV], d_res_narrow)
-    sent_a, kept_a = link.first_half(mix_both, one_both, chip_bits, order_a[0])
-    sent_b, kept_b = link.first_half(left_both, two_both, chip_bits, order_b[0])
+    sent_a, kept_a = link.first_half(mix_both_t, one_both, chip_bits, order_a[0])
+    sent_b, kept_b = link.first_half(left_both_t, two_both, chip_bits, order_b[0])
     d_pre, d_taps, kept_down, kept_gate, kept_up, act_late, _, _ = lax.optimization_barrier(
         (d_pre, d_taps, kept_down, kept_gate, kept_up, act, sent_a, sent_b)
     )

time: 397 us -> 397 us (level)
    optimization_barrier x0 -> x3, local copies, waits for them, and re-layouts: none -> 4.57 us  [the longest x2 4.37 us: on_device(): in_both_t, act_t = lax.optimization_barrier((in_both.T, act.T))]
where the time goes in v1:
time: 397 us; the launch traced here: 390 us
  waiting for transfers between devices  161 us (41%)
  starting transfers between devices  58.9 us (15%)
  matrix products  49.5 us (12%)
  local copies, waits for them, and re-layouts  49.4 us (12%)
  other arithmetic  34 us (9%)
  Pallas kernels  21.2 us (5%)
  between operations  15.4 us (4%)
    ppermute x48, waiting for transfers between devices, swap(): return lax.ppermute(array, 'fsdp', [(i, i ^ 1 << p) for i in range(self.n)])  147 us
    ppermute x48, starting transfers between devices, swap(): return lax.ppermute(array, 'fsdp', [(i, i ^ 1 << p) for i in range(self.n)])  55.6 us
    dot_general x15, matrix products, mm(): return jnp.dot(a, b, preferred_element_type=F32)  31.8 us
    dot_general x5, matrix products, mm_t(): lax.dot_general(a, b, (((1,), (1,)), ((), ())), preferred_element_type=F32)  16.5 us
    select_n x10, other arithmetic, spread(): rows = jnp.where(place == self.bit(p), split(rows), split(other))  15.9 us
    unnamed x103, local copies, waits for them, and re-layouts  14.8 us
    all_gather x1, waiting for transfers between devices, on_device(): lax.all_gather(jnp.concatenate([w_query, w_key, w_value, w_gate, small_co...  14.4 us
    pallas_call x1, Pallas kernels, mixer_bwd(): pl.pallas_call(mixer_bwd_kernel, out_shape=(jax.ShapeDtypeStruct((n, QKV...  11.3 us
  transfers between devices with their start and end apart: 51, of which 20 were waited for; matrix products, arithmetic and copies ran while one was open for 27% of the time, Pallas kernels for 3%

profile of v1, /device:TPU:0, one launch (start us, length us, event | category | flops | bytes accessed | tf_op | source)
XLA Modules:
  0.0 389.7 jit_solution(18100549011966990456)
XLA Ops:
  19.7 4.0 %collective-permute-start.8 = (bf16[1,64,2816]{2,1,0:T(8,128)(2,1)S(1)}, bf16[1,64,2816]{2,1,0:T(8,128)(2,1)S(1)}, u32[]{:S(2)}, u32[]{:S(2)}) collective-permute-start(bf16[1,64,2816]{2,1,0:T(8,128)(2,1)S(1)} %get-tuple-element.159), channel_id=1, source_target_pairs={{0,16},{1,17},{2,18},{3,19},{4,20},{5,21},{6,22},{7,23},{8,24},{9,... | collective-permute-start | bytes 1081352 | tf_op jit(solution)/shard_map/ppermute | solution.py:298
  25.8 24.6 %collective-permute-done.8 = bf16[1,64,2816]{2,1,0:T(8,128)(2,1)S(1)} collective-permute-done((bf16[1,64,2816]{2,1,0:T(8,128)(2,1)S(1)}, bf16[1,64,2816]{2,1,0:T(8,128)(2,1)S(1)}, u32[]{:S(2)}, u32[]{:S(2)}) %collective-permute-start.8) | collective-permute-done | bytes 360480 | tf_op jit(solution)/shard_map/ppermute | solution.py:298
  52.7 7.8 %collective-permute-done.3 = bf16[1,176,1024]{2,1,0:T(8,128)(2,1)S(1)} collective-permute-done((bf16[1,176,1024]{2,1,0:T(8,128)(2,1)S(1)}, bf16[1,176,1024]{2,1,0:T(8,128)(2,1)S(1)}, u32[]{:S(2)}, u32[]{:S(2)}) %collective-permute-start.3) | collective-permute-done | bytes 360480 | tf_op jit(solution)/shard_map/ppermute | solution.py:298
  62.5 18.0 %collective-permute-done.9 = bf16[2,64,2816]{2,1,0:T(8,128)(2,1)S(1)} collective-permute-done((bf16[2,64,2816]{2,1,0:T(8,128)(2,1)S(1)}, bf16[2,64,2816]{2,1,0:T(8,128)(2,1)S(1)}, u32[]{:S(2)}, u32[]{:S(2)}) %collective-permute-start.9) | collective-permute-done | bytes 720928 | tf_op jit(solution)/shard_map/ppermute | solution.py:298
  89.3 21.3 %collective-permute-done.12 = bf16[4,64,1408]{2,1,0:T(8,128)(2,1)} collective-permute-done((bf16[4,64,1408]{2,1,0:T(8,128)(2,1)S(1)}, bf16[4,64,1408]{2,1,0:T(8,128)(2,1)}, u32[]{:S(2)}, u32[]{:S(2)}) %collective-permute-start.12) | collective-permute-done | bytes 720928 | tf_op jit(solution)/shard_map/ppermute | solution.py:298
  110.5 2.5 bitcast_select_fusion.3
  115.7 2.7 bitcast_select_fusion.4
  119.3 14.4 %all-gather.2.cloned.1.call-done = bf16[1024,4224]{1,0:T(8,128)(2,1)} async-done(((bf16[32,4224]{1,0:T(8,128)(2,1)}), bf16[1024,4224]{1,0:T(8,128)(2,1)}) %all-gather.2.cloned.1.call-update) | async-done | bytes 8650768 | tf_op jit(solution)/shard_map/all_gather | solution.py:397
  136.4 5.2 %fusion.2.pre_ref = f32[128,3200]{1,0:T(8,128)} fusion(bf16[128,1024]{1,0:T(8,128)(2,1)} %fusion.26, bf16[1024,4224]{1,0:T(8,128)(2,1)} %all-gather.2.cloned.1.call-done), kind=kOutput, calls=%fused_computation.2 | convolution fusion | flops 838860800 | bytes 8454144 | tf_op jit(solution)/shard_map/dot_general | solution.py:28
  145.9 10.0 %mixer_fwd.1 = (bf16[128,1024]{1,0:T(8,128)(2,1)}, f32[128,512]{1,0:T(8,128)}, f32[128,1024]{1,0:T(8,128)}, f32[128,1024]{1,0:T(8,128)}) custom-call(s32[1,4]{1,0:T(1,128)} %len_ref.3, s32[1,4]{1,0:T(1,128)} %off_ref.3, f32[128,3200]{1,0:T(8,128)} %fusion.2.pre_ref, f32[4,2048]{1,0:T(4,128)} %bitcast.302, f32[1,256]{1,0:T(1,128)} %reshape.391.gain_ref, ...), custom_call_target="tpu_custom_call" | custom-call | tf_op jit(solution)/shard_map/mixer_fwd/pallas_call | solution.py:254
  159.9 3.4 bitcast_select_fusion.2
  178.8 3.3 constant_dynamic-slice_fusion.9
  184.0 5.1 %multiply_convert_fusion = (bf16[256,1408]{1,0:T(8,128)(2,1)}, bf16[256,1408]{1,0:T(8,128)(2,1)S(1)}, bf16[256,1408]{1,0:T(8,128)(2,1)S(1)}) fusion(f32[256,1408]{1,0:T(8,128)} %get-tuple-element.177, f32[256,1408]{1,0:T(8,128)} %copy-done.17, bf16[1408,1024]{1,0:T(8,128)(2,1)} %bitcast_select_fusion.2, bf16[128,1024]{1,0:T(8,128)(2,1)} %collective-permute-done, ...), kind=kOutput, calls=%fused_computation.38 | convolution fusion | flops 744652800 | bytes 8454144 | tf_op jit(solution)/shard_map/dot_general | solution.py:32
  193.3 2.7 convolution_convert_fusion.2
  206.0 3.2 fusion.4.dmix_ref
  209.4 11.3 %mixer_bwd.1 = (bf16[128,3200]{1,0:T(8,128)(2,1)}, f32[4,2048]{1,0:T(4,128)}, f32[1,256]{1,0:T(1,128)}, f32[2,128]{1,0:T(2,128)}) custom-call(s32[1,4]{1,0:T(1,128)} %len_ref.3, s32[1,4]{1,0:T(1,128)} %off_ref.3, f32[128,3200]{1,0:T(8,128)} %fusion.2.pre_ref, f32[4,2048]{1,0:T(4,128)} %bitcast.303, f32[1,256]{1,0:T(1,128)} %reshape.391.gain_ref, ...), custom_call_target="tpu_custom_call" | custom-call | tf_op jit(solution)/shard_map/mixer_bwd/pallas_call | solution.py:271
  234.5 6.2 %fusion.32 = (f32[1024]{0:T(1024)S(1)}, f32[128]{0:T(128)S(1)}, f32[128,1024]{1,0:T(8,128)}) fusion(bf16[128,1024]{1,0:T(8,128)(2,1)S(1)} %copy-done.6, f32[128]{0:T(128)S(1)} %get-tuple-element.171, f32[1024]{0:T(1024)S(1)} %get-tuple-element.128, bf16[128,3200]{1,0:T(8,128)(2,1)} %get-tuple-element.51, bf16[1024,4224]{1,0:T(8,128)(2,1)} %all-gather.2.cloned.1.call-done), kind=kOutput, calls=%fused_computation.75 | convolution fusion | flops 839777152 | bytes 8168448 | tf_op jit(solution)/shard_map/dot_general | solution.py:32
  243.3 5.6 %collective-permute-start.21 = (f32[2,2,2,8,128]{4,3,2,1,0:T(8,128)S(1)}, f32[2,2,2,8,128]{4,3,2,1,0:T(8,128)S(1)}, u32[]{:S(2)}, u32[]{:S(2)}) collective-permute-start(f32[2,2,2,8,128]{4,3,2,1,0:T(8,128)S(1)} %dynamic-slice_bitcast_fusion.21), channel_id=1, source_target_pairs={{0,8},{1,9},{2,10},{3,11},{4,12},{5,13},{6,14},{7,15},{8,0},{9,1},... | collective-permute-start | bytes 98312 | tf_op jit(solution)/shard_map/ppermute | solution.py:298
  251.5 3.7 collective-permute-start.22
  255.3 2.8 fusion.74
  259.0 22.8 %collective-permute-done.22 = f32[2,2,8,128]{3,2,1,0:T(8,128)S(1)} collective-permute-done((f32[2,2,8,128]{3,2,1,0:T(8,128)S(1)}, f32[2,2,8,128]{3,2,1,0:T(8,128)S(1)}, u32[]{:S(2)}, u32[]{:S(2)}) %collective-permute-start.22) | collective-permute-done | bytes 16416 | tf_op jit(solution)/shard_map/ppermute | solution.py:298
  298.9 4.2 %collective-permute-start.36 = (bf16[2,2,64,1408]{3,2,1,0:T(8,128)(2,1)S(1)}, bf16[2,2,64,1408]{3,2,1,0:T(8,128)(2,1)S(1)}, u32[]{:S(2)}, u32[]{:S(2)}) collective-permute-start(bf16[2,2,64,1408]{3,2,1,0:T(8,128)(2,1)S(1)} %dynamic-slice_bitcast_fusion.2), channel_id=1, source_target_pairs={{0,8},{1,9},{2,10},{3,11},{4,12},{5,13},{6,14},{7,15},{8,0},{9,1},... | collective-permute-start | bytes 2162696 | tf_op jit(solution)/shard_map/ppermute | solution.py:298
  309.1 6.4 %collective-permute-done.25 = bf16[512,1024]{1,0:T(8,128)(2,1)} collective-permute-done((bf16[512,1024]{1,0:T(8,128)(2,1)}, bf16[512,1024]{1,0:T(8,128)(2,1)}, u32[]{:S(2)}, u32[]{:S(2)}) %collective-permute-start.25) | collective-permute-done | bytes 1048608 | tf_op jit(solution)/shard_map/ppermute | solution.py:298
  321.3 3.4 collective-permute-start.37
  324.7 10.9 %collective-permute-done.41 = bf16[2,2,64,1408]{3,2,1,0:T(8,128)(2,1)S(1)} collective-permute-done((bf16[2,2,64,1408]{3,2,1,0:T(8,128)(2,1)S(1)}, bf16[2,2,64,1408]{3,2,1,0:T(8,128)(2,1)S(1)}, u32[]{:S(2)}, u32[]{:S(2)}) %collective-permute-start.41) | collective-permute-done | bytes 720928 | tf_op jit(solution)/shard_map/ppermute | solution.py:298
  335.9 4.2 %collective-permute-start.42 = (bf16[2,64,1408]{2,1,0:T(8,128)(2,1)S(1)}, bf16[2,64,1408]{2,1,0:T(8,128)(2,1)S(1)}, u32[]{:S(2)}, u32[]{:S(2)}) collective-permute-start(bf16[2,64,1408]{2,1,0:T(8,128)(2,1)S(1)} %dynamic-slice_bitcast_fusion.7), channel_id=1, source_target_pairs={{0,8},{1,9},{2,10},{3,11},{4,12},{5,13},{6,14},{7,15},{8,0},{9,1},... | collective-permute-start | bytes 1081352 | tf_op jit(solution)/shard_map/ppermute | solution.py:298
  341.2 5.3 %collective-permute-done.26 = bf16[2,2,64,1024]{3,2,1,0:T(8,128)(2,1)S(1)} collective-permute-done((bf16[2,2,64,1024]{3,2,1,0:T(8,128)(2,1)S(1)}, bf16[2,2,64,1024]{3,2,1,0:T(8,128)(2,1)S(1)}, u32[]{:S(2)}, u32[]{:S(2)}) %collective-permute-start.26) | collective-permute-done | bytes 524320 | tf_op jit(solution)/shard_map/ppermute | solution.py:298
  346.7 3.8 collective-permute-start.27
  354.1 3.6 collective-permute-done.27
  359.0 4.6 %collective-permute-done.32 = bf16[2,64,1024]{2,1,0:T(8,128)(2,1)S(1)} collective-permute-done((bf16[2,64,1024]{2,1,0:T(8,128)(2,1)S(1)}, bf16[2,64,1024]{2,1,0:T(8,128)(2,1)S(1)}, u32[]{:S(2)}, u32[]{:S(2)}) %collective-permute-start.32) | collective-permute-done | bytes 262176 | tf_op jit(solution)/shard_map/ppermute | solution.py:298
  364.0 2.6 collective-permute-done.43
  366.8 9.1 %collective-permute-done.28 = bf16[64,1024]{1,0:T(8,128)(2,1)S(1)} collective-permute-done((bf16[64,1024]{1,0:T(8,128)(2,1)S(1)}, bf16[64,1024]{1,0:T(8,128)(2,1)S(1)}, u32[]{:S(2)}, u32[]{:S(2)}) %collective-permute-start.28) | collective-permute-done | bytes 131104 | tf_op jit(solution)/shard_map/ppermute | solution.py:298
  (352 shorter events, 135.8 us)
Async XLA Ops:
  7.2 126.5 %all-gather.2.cloned.1.call-start = ((), (), s32[]{:S(2)}) async-start(), calls=%async_computation | async-start | bytes 8921088 | tf_op jit(solution)/shard_map/all_gather | solution.py:397
  19.7 30.7 %collective-permute-start.8 = (bf16[1,64,2816]{2,1,0:T(8,128)(2,1)S(1)}, bf16[1,64,2816]{2,1,0:T(8,128)(2,1)S(1)}, u32[]{:S(2)}, u32[]{:S(2)}) collective-permute-start(bf16[1,64,2816]{2,1,0:T(8,128)(2,1)S(1)} %get-tuple-element.159), channel_id=1, source_target_pairs={{0,16},{1,17},{2,18},{3,19},{4,20},{5,21},{6,22},{7,23},{8,24},{9,... | collective-permute-start | bytes 1081352 | tf_op jit(solution)/shard_map/ppermute | solution.py:298
  23.8 27.0 %collective-permute-start.2 = (bf16[176,1024]{1,0:T(8,128)(2,1)S(1)}, bf16[176,1024]{1,0:T(8,128)(2,1)S(1)}, u32[]{:S(2)}, u32[]{:S(2)}) collective-permute-start(bf16[176,1024]{1,0:T(8,128)(2,1)S(1)} %pad_maximum_fusion.4), channel_id=1, source_target_pairs={{0,16},{2,18},{4,20},{6,22},{8,24},{10,26},{12,28},{14,30},{17,1},... | collective-permute-start | bytes 1081352 | tf_op jit(solution)/shard_map/ppermute | solution.py:303
  50.5 30.0 %collective-permute-start.9 = (bf16[2,64,2816]{2,1,0:T(8,128)(2,1)S(1)}, bf16[2,64,2816]{2,1,0:T(8,128)(2,1)S(1)}, u32[]{:S(2)}, u32[]{:S(2)}) collective-permute-start(bf16[2,64,2816]{2,1,0:T(8,128)(2,1)S(1)} %broadcast_select_fusion.1), channel_id=1, source_target_pairs={{0,8},{1,9},{2,10},{3,11},{4,12},{5,13},{6,14},{7,15},{8,0},{9,1},... | collective-permute-start | bytes 2162696 | tf_op jit(solution)/shard_map/ppermute | solution.py:298
  60.7 27.0 %collective-permute-start.4 = (bf16[2,176,1024]{2,1,0:T(8,128)(2,1)S(1)}, bf16[2,176,1024]{2,1,0:T(8,128)(2,1)}, u32[]{:S(2)}, u32[]{:S(2)}) collective-permute-start(bf16[2,176,1024]{2,1,0:T(8,128)(2,1)S(1)} %broadcast_select_fusion.2), channel_id=1, source_target_pairs={{0,4},{1,5},{2,6},{3,7},{4,0},{5,1},{6,2},{7,3},{8,12},{9,13},{10,... | collective-permute-start | bytes 2162696 | tf_op jit(solution)/shard_map/ppermute | solution.py:298
  81.8 28.8 %collective-permute-start.12 = (bf16[4,64,1408]{2,1,0:T(8,128)(2,1)S(1)}, bf16[4,64,1408]{2,1,0:T(8,128)(2,1)}, u32[]{:S(2)}, u32[]{:S(2)}) collective-permute-start(bf16[4,64,1408]{2,1,0:T(8,128)(2,1)S(1)} %get-tuple-element.133), channel_id=1, source_target_pairs={{0,2},{1,3},{2,0},{3,1},{4,6},{5,7},{6,4},{7,5},{8,10},{9,11},{10,... | collective-permute-start | bytes 2162696 | tf_op jit(solution)/shard_map/ppermute | solution.py:298
  83.6 32.1 %collective-permute-start.10 = (bf16[4,64,1408]{2,1,0:T(8,128)(2,1)}, bf16[4,64,1408]{2,1,0:T(8,128)(2,1)}, u32[]{:S(2)}, u32[]{:S(2)}) collective-permute-start(bf16[4,64,1408]{2,1,0:T(8,128)(2,1)} %get-tuple-element.132), channel_id=1, source_target_pairs={{0,4},{1,5},{2,6},{3,7},{4,0},{5,1},{6,2},{7,3},{8,12},{9,13},{10,... | collective-permute-start | bytes 2162696 | tf_op jit(solution)/shard_map/ppermute | solution.py:298
  86.0 98.0 %collective-permute-start = (bf16[128,1024]{1,0:T(8,128)(2,1)}, bf16[128,1024]{1,0:T(8,128)(2,1)}, u32[]{:S(2)}, u32[]{:S(2)}) collective-permute-start(bf16[128,1024]{1,0:T(8,128)(2,1)} %fusion.38), channel_id=1, source_target_pairs={{0,1},{1,0},{2,3},{3,2},{4,5},{5,4},{6,7},{7,6},{8,9},{9,8},{10,11... | collective-permute-start | bytes 786440 | tf_op jit(solution)/shard_map/ppermute | solution.py:298
  89.2 70.7 %collective-permute-start.5 = (bf16[4,176,1024]{2,1,0:T(8,128)(2,1)S(1)}, bf16[4,176,1024]{2,1,0:T(8,128)(2,1)}, u32[]{:S(2)}, u32[]{:S(2)}) collective-permute-start(bf16[4,176,1024]{2,1,0:T(8,128)(2,1)S(1)} %bitcast_select_fusion.6), channel_id=1, source_target_pairs={{0,8},{1,9},{2,10},{3,11},{4,12},{5,13},{6,14},{7,15},{8,0},{9,1},... | collective-permute-start | bytes 4325384 | tf_op jit(solution)/shard_map/ppermute | solution.py:298
  113.0 50.2 %collective-permute-start.13 = (bf16[8,64,1408]{2,1,0:T(8,128)(2,1)}, bf16[8,64,1408]{2,1,0:T(8,128)(2,1)}, u32[]{:S(2)}, u32[]{:S(2)}) collective-permute-start(bf16[8,64,1408]{2,1,0:T(8,128)(2,1)} %bitcast_select_fusion.3), channel_id=1, source_target_pairs={{0,4},{1,5},{2,6},{3,7},{4,0},{5,1},{6,2},{7,3},{8,12},{9,13},{10,... | collective-permute-start | bytes 4325384 | tf_op jit(solution)/shard_map/ppermute | solution.py:298
  118.3 46.8 %collective-permute-start.11 = (bf16[8,64,1408]{2,1,0:T(8,128)(2,1)}, bf16[8,64,1408]{2,1,0:T(8,128)(2,1)}, u32[]{:S(2)}, u32[]{:S(2)}) collective-permute-start(bf16[8,64,1408]{2,1,0:T(8,128)(2,1)} %bitcast_select_fusion.4), channel_id=1, source_target_pairs={{0,2},{1,3},{2,0},{3,1},{4,6},{5,7},{6,4},{7,5},{8,10},{9,11},{10,... | collective-permute-start | bytes 4325384 | tf_op jit(solution)/shard_map/ppermute | solution.py:298
  167.3 35.4 %collective-permute-start.15 = (bf16[128,1024]{1,0:T(8,128)(2,1)}, bf16[128,1024]{1,0:T(8,128)(2,1)}, u32[]{:S(2)}, u32[]{:S(2)}) collective-permute-start(bf16[128,1024]{1,0:T(8,128)(2,1)} %fusion.26), channel_id=1, source_target_pairs={{0,1},{1,0},{2,3},{3,2},{4,5},{5,4},{6,7},{7,6},{8,9},{9,8},{10,11... | collective-permute-start | bytes 786440 | tf_op jit(solution)/shard_map/ppermute | solution.py:298
  248.9 48.0 %collective-permute-start.35 = (bf16[512,1408]{1,0:T(8,128)(2,1)}, bf16[512,1408]{1,0:T(8,128)(2,1)}, u32[]{:S(2)}, u32[]{:S(2)}) collective-permute-start(bf16[512,1408]{1,0:T(8,128)(2,1)} %convolution_convert_fusion.1), channel_id=1, source_target_pairs={{0,4},{1,5},{2,6},{3,7},{4,0},{5,1},{6,2},{7,3},{8,12},{9,13},{10,... | collective-permute-start | bytes 4325384 | tf_op jit(solution)/shard_map/ppermute | solution.py:298
  250.2 52.9 %collective-permute-start.40 = (bf16[512,1408]{1,0:T(8,128)(2,1)}, bf16[512,1408]{1,0:T(8,128)(2,1)}, u32[]{:S(2)}, u32[]{:S(2)}) collective-permute-start(bf16[512,1408]{1,0:T(8,128)(2,1)} %convolution_convert_fusion), channel_id=1, source_target_pairs={{0,2},{1,3},{2,0},{3,1},{4,6},{5,7},{6,4},{7,5},{8,10},{9,11},{10,... | collective-permute-start | bytes 4325384 | tf_op jit(solution)/shard_map/ppermute | solution.py:298
  250.3 56.2 %collective-permute-start.45 = (bf16[704,1024]{1,0:T(8,128)(2,1)}, bf16[704,1024]{1,0:T(8,128)(2,1)}, u32[]{:S(2)}, u32[]{:S(2)}) collective-permute-start(bf16[704,1024]{1,0:T(8,128)(2,1)} %convolution_convert_fusion.2), channel_id=1, source_target_pairs={{0,8},{1,9},{2,10},{3,11},{4,12},{5,13},{6,14},{7,15},{8,0},{9,1},... | collective-permute-start | bytes 4325384 | tf_op jit(solution)/shard_map/ppermute | solution.py:298
  251.5 30.3 %collective-permute-start.22 = (f32[2,2,8,128]{3,2,1,0:T(8,128)S(1)}, f32[2,2,8,128]{3,2,1,0:T(8,128)S(1)}, u32[]{:S(2)}, u32[]{:S(2)}) collective-permute-start(f32[2,2,8,128]{3,2,1,0:T(8,128)S(1)} %dynamic-slice_bitcast_fusion.22), channel_id=1, source_target_pairs={{0,16},{1,17},{2,18},{3,19},{4,20},{5,21},{6,22},{7,23},{8,24},{9,... | collective-permute-start | bytes 49160 | tf_op jit(solution)/shard_map/ppermute | solution.py:298
  259.0 35.1 %collective-permute-start.19 = (f32[128,1024]{1,0:T(8,128)}, f32[128,1024]{1,0:T(8,128)}, u32[]{:S(2)}, u32[]{:S(2)}) collective-permute-start(f32[128,1024]{1,0:T(8,128)} %slice.133), channel_id=1, source_target_pairs={{0,1},{1,0},{2,3},{3,2},{4,5},{5,4},{6,7},{7,6},{8,9},{9,8},{10,11... | collective-permute-start | bytes 1572872 | tf_op jit(solution)/shard_map/ppermute | solution.py:298
  289.1 26.4 %collective-permute-start.25 = (bf16[512,1024]{1,0:T(8,128)(2,1)}, bf16[512,1024]{1,0:T(8,128)(2,1)}, u32[]{:S(2)}, u32[]{:S(2)}) collective-permute-start(bf16[512,1024]{1,0:T(8,128)(2,1)} %convolution_convert_fusion.4), channel_id=1, source_target_pairs={{0,2},{1,3},{2,0},{3,1},{4,6},{5,7},{6,4},{7,5},{8,10},{9,11},{10,... | collective-permute-start | bytes 3145736 | tf_op jit(solution)/shard_map/ppermute | solution.py:298
  294.1 26.0 %collective-permute-start.30 = (bf16[512,1024]{1,0:T(8,128)(2,1)S(1)}, bf16[512,1024]{1,0:T(8,128)(2,1)S(1)}, u32[]{:S(2)}, u32[]{:S(2)}) collective-permute-start(bf16[512,1024]{1,0:T(8,128)(2,1)S(1)} %copy-done.19), channel_id=1, source_target_pairs={{0,4},{1,5},{2,6},{3,7},{4,0},{5,1},{6,2},{7,3},{8,12},{9,13},{10,... | collective-permute-start | bytes 3145736 | tf_op jit(solution)/shard_map/ppermute | solution.py:298
  298.9 22.2 %collective-permute-start.36 = (bf16[2,2,64,1408]{3,2,1,0:T(8,128)(2,1)S(1)}, bf16[2,2,64,1408]{3,2,1,0:T(8,128)(2,1)S(1)}, u32[]{:S(2)}, u32[]{:S(2)}) collective-permute-start(bf16[2,2,64,1408]{3,2,1,0:T(8,128)(2,1)S(1)} %dynamic-slice_bitcast_fusion.2), channel_id=1, source_target_pairs={{0,8},{1,9},{2,10},{3,11},{4,12},{5,13},{6,14},{7,15},{8,0},{9,1},... | collective-permute-start | bytes 2162696 | tf_op jit(solution)/shard_map/ppermute | solution.py:298
  305.1 30.5 %collective-permute-start.41 = (bf16[2,2,64,1408]{3,2,1,0:T(8,128)(2,1)S(1)}, bf16[2,2,64,1408]{3,2,1,0:T(8,128)(2,1)S(1)}, u32[]{:S(2)}, u32[]{:S(2)}) collective-permute-start(bf16[2,2,64,1408]{3,2,1,0:T(8,128)(2,1)S(1)} %dynamic-slice_bitcast_fusion.1), channel_id=1, source_target_pairs={{0,4},{1,5},{2,6},{3,7},{4,0},{5,1},{6,2},{7,3},{8,12},{9,13},{10,... | collective-permute-start | bytes 2162696 | tf_op jit(solution)/shard_map/ppermute | solution.py:298
  308.7 31.4 %collective-permute-start.46 = (bf16[2,176,1024]{2,1,0:T(8,128)(2,1)S(1)}, bf16[2,176,1024]{2,1,0:T(8,128)(2,1)S(1)}, u32[]{:S(2)}, u32[]{:S(2)}) collective-permute-start(bf16[2,176,1024]{2,1,0:T(8,128)(2,1)S(1)} %dynamic-slice_bitcast_fusion), channel_id=1, source_target_pairs={{0,2},{1,3},{2,0},{3,1},{4,6},{5,7},{6,4},{7,5},{8,10},{9,11},{10,... | collective-permute-start | bytes 2162696 | tf_op jit(solution)/shard_map/ppermute | solution.py:298
  317.3 29.1 %collective-permute-start.26 = (bf16[2,2,64,1024]{3,2,1,0:T(8,128)(2,1)S(1)}, bf16[2,2,64,1024]{3,2,1,0:T(8,128)(2,1)S(1)}, u32[]{:S(2)}, u32[]{:S(2)}) collective-permute-start(bf16[2,2,64,1024]{3,2,1,0:T(8,128)(2,1)S(1)} %dynamic-slice_bitcast_fusion.4), channel_id=1, source_target_pairs={{0,4},{1,5},{2,6},{3,7},{4,0},{5,1},{6,2},{7,3},{8,12},{9,13},{10,... | collective-permute-start | bytes 1572872 | tf_op jit(solution)/shard_map/ppermute | solution.py:298
  320.7 29.8 %collective-permute-start.31 = (bf16[2,2,64,1024]{3,2,1,0:T(8,128)(2,1)S(1)}, bf16[2,2,64,1024]{3,2,1,0:T(8,128)(2,1)S(1)}, u32[]{:S(2)}, u32[]{:S(2)}) collective-permute-start(bf16[2,2,64,1024]{3,2,1,0:T(8,128)(2,1)S(1)} %dynamic-slice_bitcast_fusion.3), channel_id=1, source_target_pairs={{0,2},{1,3},{2,0},{3,1},{4,6},{5,7},{6,4},{7,5},{8,10},{9,11},{10,... | collective-permute-start | bytes 1572872 | tf_op jit(solution)/shard_map/ppermute | solution.py:298
  321.3 29.5 %collective-permute-start.37 = (bf16[2,64,1408]{2,1,0:T(8,128)(2,1)S(1)}, bf16[2,64,1408]{2,1,0:T(8,128)(2,1)S(1)}, u32[]{:S(2)}, u32[]{:S(2)}) collective-permute-start(bf16[2,64,1408]{2,1,0:T(8,128)(2,1)S(1)} %dynamic-slice_bitcast_fusion.8), channel_id=1, source_target_pairs={{0,16},{1,17},{2,18},{3,19},{4,20},{5,21},{6,22},{7,23},{8,24},{9,... | collective-permute-start | bytes 1081352 | tf_op jit(solution)/shard_map/ppermute | solution.py:298
  335.9 15.4 %collective-permute-start.42 = (bf16[2,64,1408]{2,1,0:T(8,128)(2,1)S(1)}, bf16[2,64,1408]{2,1,0:T(8,128)(2,1)S(1)}, u32[]{:S(2)}, u32[]{:S(2)}) collective-permute-start(bf16[2,64,1408]{2,1,0:T(8,128)(2,1)S(1)} %dynamic-slice_bitcast_fusion.7), channel_id=1, source_target_pairs={{0,8},{1,9},{2,10},{3,11},{4,12},{5,13},{6,14},{7,15},{8,0},{9,1},... | collective-permute-start | bytes 1081352 | tf_op jit(solution)/shard_map/ppermute | solution.py:298
  351.4 15.2 %collective-permute-start.43 = (bf16[64,1408]{1,0:T(8,128)(2,1)S(1)}, bf16[64,1408]{1,0:T(8,128)(2,1)S(1)}, u32[]{:S(2)}, u32[]{:S(2)}) collective-permute-start(bf16[64,1408]{1,0:T(8,128)(2,1)S(1)} %dynamic-slice_bitcast_fusion.13), channel_id=1, source_target_pairs={{0,16},{1,17},{2,18},{3,19},{4,20},{5,21},{6,22},{7,23},{8,24},{9,... | collective-permute-start | bytes 540680 | tf_op jit(solution)/shard_map/ppermute | solution.py:298
  352.8 24.6 %collective-permute-start.48 = (bf16[176,1024]{1,0:T(8,128)(2,1)S(1)}, bf16[176,1024]{1,0:T(8,128)(2,1)S(1)}, u32[]{:S(2)}, u32[]{:S(2)}) collective-permute-start(bf16[176,1024]{1,0:T(8,128)(2,1)S(1)} %fusion.23), channel_id=1, source_target_pairs={{1,17},{3,19},{5,21},{7,23},{9,25},{11,27},{13,29},{15,31},{16,0},... | collective-permute-start | bytes 1081352 | tf_op jit(solution)/shard_map/ppermute | solution.py:303
  357.8 18.1 %collective-permute-start.28 = (bf16[64,1024]{1,0:T(8,128)(2,1)S(1)}, bf16[64,1024]{1,0:T(8,128)(2,1)S(1)}, u32[]{:S(2)}, u32[]{:S(2)}) collective-permute-start(bf16[64,1024]{1,0:T(8,128)(2,1)S(1)} %dynamic-slice_bitcast_fusion.19), channel_id=1, source_target_pairs={{0,16},{1,17},{2,18},{3,19},{4,20},{5,21},{6,22},{7,23},{8,24},{9,... | collective-permute-start | bytes 393224 | tf_op jit(solution)/shard_map/ppermute | solution.py:298
  363.8 13.5 %collective-permute-start.33 = (bf16[64,1024]{1,0:T(8,128)(2,1)S(1)}, bf16[64,1024]{1,0:T(8,128)(2,1)S(1)}, u32[]{:S(2)}, u32[]{:S(2)}) collective-permute-start(bf16[64,1024]{1,0:T(8,128)(2,1)S(1)} %dynamic-slice_bitcast_fusion.17), channel_id=1, source_target_pairs={{0,16},{1,17},{2,18},{3,19},{4,20},{5,21},{6,22},{7,23},{8,24},{9,... | collective-permute-start | bytes 393224 | tf_op jit(solution)/shard_map/ppermute | solution.py:298
  363.9 14.3 %collective-permute-start.39 = (f32[32,1408]{1,0:T(8,128)S(1)}, f32[32,1408]{1,0:T(8,128)S(1)}, u32[]{:S(2)}, u32[]{:S(2)}) collective-permute-start(f32[32,1408]{1,0:T(8,128)S(1)} %dynamic-slice_bitcast_fusion.14), channel_id=1, source_target_pairs={{0,1},{1,0},{2,3},{3,2},{4,5},{5,4},{6,7},{7,6},{8,9},{9,8},{10,11... | collective-permute-start | bytes 540680 | tf_op jit(solution)/shard_map/ppermute | solution.py:298
  366.7 13.7 %collective-permute-start.44 = (f32[32,1408]{1,0:T(8,128)S(1)}, f32[32,1408]{1,0:T(8,128)S(1)}, u32[]{:S(2)}, u32[]{:S(2)}) collective-permute-start(f32[32,1408]{1,0:T(8,128)S(1)} %dynamic-slice_bitcast_fusion.12), channel_id=1, source_target_pairs={{0,1},{1,0},{2,3},{3,2},{4,5},{5,4},{6,7},{7,6},{8,9},{9,8},{10,11... | collective-permute-start | bytes 540680 | tf_op jit(solution)/shard_map/ppermute | solution.py:298
  (61 other events, 456.0 us)
Sparse Core Ops, SparseCore 0:
  16.2 117.4 all-gather.1
